TPU v7x, 128 devices: a whole 4x4x4 slice. The times are simulated.
128 devices in a mesh: row: 16 (over y, x), col: 8 (over z, core).
Axes of the slice: x: 4, y: 4, z: 4, core: 2. Of those that a mesh axis runs over, the one named last changes fastest.
Arguments:
- x_blocks: bfloat16 [128, 16, 256, 256], P('row', 'col'), may hold values from -0.75 to 0.75, as said below
- x_cols: int32 [128, 16], P('row', 'col'), may hold values from -1 to 127, as said below
- out_cols: int32 [128, 32], P('row', 'col'), may hold values from 0 to 127, as said below
- branch_flag: int32 [128], P('row'), may hold values from 0 to 1
Outputs:
- purified: bfloat16 [128, 32, 256, 256], P('row', 'col')
- trace: float32 [1], replicated
Inputs may be any that keep to these rules, and one draw needn't show every extreme that they name: `x_cols`: slot c * 2 + s of block row i holds -1 or a block column in c * 16 to (c + 1) * 16 - 1; the filled columns of one block row are distinct. The pattern is symmetric: block row i names column j exactly when block row j names column i. The rows of one device hold at most 13 filled slots together, and the rows of some device hold exactly 13. `x_blocks`: the stored block of position (j, i) is the transpose of the stored block of position (i, j); stored diagonal blocks are symmetric. `out_cols`: slot c * 4 + o of block row i holds a block column in c * 16 to (c + 1) * 16 - 1, distinct within one block row; column i is always among the slots of block row i. `branch_flag`: entry i is 0 where block row i takes X times X, 1 where it takes 2 X minus X times X.
All inputs are finite; a program needn't handle non-finite values.
Results may differ from a plain program's by a relative error of at most 0.001.
Values may be sent and summed in bfloat16 or wider, within the bound.
A program may use at most 192 MiB of HBM per device.

v0:
```python
import jax
import jax.numpy as jnp
from jax import lax
from jax.sharding import PartitionSpec as P


def per_device(x_blocks, x_cols, out_cols, branch_flag):
    rows = x_cols.shape[0]
    slots = x_cols.shape[1]
    block = x_blocks.shape[-1]
    kept = out_cols.shape[1]
    filled = x_cols >= 0
    cleared = jnp.where(filled[:, :, None, None], x_blocks, jnp.zeros_like(x_blocks))
    flag_rows = branch_flag == 1
    base_row = lax.axis_index("row") * rows
    left_blocks, left_cols = (
        lax.all_gather(cleared, "col", axis=1, tiled=True),
        lax.all_gather(x_cols, "col", axis=1, tiled=True),
    )
    right_blocks, right_cols = (
        lax.all_gather(cleared, "row", axis=0, tiled=True),
        lax.all_gather(x_cols, "row", axis=0, tiled=True),
    )

    def fetch(local):
        entries = left_cols[local]
        live = entries >= 0
        source_rows = jnp.where(live, entries, 0)
        fetched = right_blocks[source_rows]
        fetched_cols = jnp.where(live[:, None], right_cols[source_rows], -1)
        return (left_blocks[local], fetched, fetched_cols)

    def one_row(local):
        lhs, fetched, fetched_cols = fetch(local)
        width = fetched_cols.shape[0] * fetched_cols.shape[1]
        products = jnp.einsum("exy,esyz->esxz", lhs, fetched, preferred_element_type=jnp.float32)
        targets = out_cols[local]
        match = (
            (fetched_cols[None, :, :] == targets[:, None, None])
            .astype(jnp.float32)
            .reshape(kept, width)
        )
        square = jnp.dot(
            match, products.reshape(width, block * block), precision=lax.Precision.HIGHEST
        ).reshape(kept, block, block)
        own_match = (x_cols[local][None, :] == targets[:, None]).astype(jnp.float32)
        own_blocks = cleared[local].astype(jnp.float32).reshape(slots, block * block)
        own = jnp.dot(own_match, own_blocks, precision=lax.Precision.HIGHEST).reshape(
            kept, block, block
        )
        result = jnp.where(flag_rows[local], 2.0 * own - square, square)
        diag_here = (targets == base_row + local).astype(jnp.float32)
        part = jnp.sum(diag_here * jnp.trace(result, axis1=1, axis2=2))
        return (result.astype(jnp.bfloat16), part)

    purified, parts = lax.map(one_row, jnp.arange(rows, dtype=jnp.int32))
    trace_total = lax.psum(jnp.sum(parts), ("row", "col"))
    return (purified, trace_total.reshape(1))


def solution(mesh):
    in_specs = (P("row", "col", None, None), P("row", "col"), P("row", "col"), P("row"))
    out_specs = (P("row", "col", None, None), P())
    return jax.shard_map(
        per_device, mesh=mesh, in_specs=in_specs, out_specs=out_specs, check_vma=False
    )
```

profile of v0, /device:TPU:2, one launch (start us, length us, event | category | flops | bytes accessed | tf_op | source)
XLA Modules:
  0.0 678.2 jit_solution(9202901547140222061)
XLA Ops:
  8.0 3.2 broadcast_select_fusion.1
  12.0 23.4 %all-gather.1 = s32[16,8,2]{1,2,0:T(2,128)S(1)} all-gather(s32[1,8,2]{1,2,0:T(2,128)S(1)} %bitcast.109), channel_id=1, replica_groups=mesh['row'=16,'col'=8] {'row'}, dimensions={0}, use_global_device_ids=true | all-gather | bytes 1088 | tf_op jit(solution)/shard_map/all_gather | solution.py:22
  35.6 12.1 %all-gather = s32[8,2,8]{2,1,0:T(2,128)S(1)} all-gather(s32[1,2,8]{2,1,0:T(2,128)S(1)} %bitcast.110), channel_id=1, replica_groups=mesh['row'=16,'col'=8] {'col'}, dimensions={0}, use_global_device_ids=true | all-gather | bytes 576 | tf_op jit(solution)/shard_map/all_gather | solution.py:18
  47.9 51.0 %all-gather.7.cloned.1.call-done = bf16[8,16,256,256]{3,2,1,0:T(8,128)(2,1)} async-done(((bf16[8,2,256,256]{3,2,1,0:T(8,128)(2,1)}), bf16[8,16,256,256]{3,2,1,0:T(8,128)(2,1)}) %all-gather.7.cloned.1.call-update) | async-done | bytes 16777232 | tf_op jit(solution)/shard_map/all_gather | solution.py:17
  98.9 199.4 %all-gather.5.cloned.1.call-done = bf16[128,2,256,256]{3,2,1,0:T(8,128)(2,1)} async-done(((bf16[8,2,256,256]{3,2,1,0:T(8,128)(2,1)}), bf16[128,2,256,256]{3,2,1,0:T(8,128)(2,1)}) %all-gather.5.cloned.1.call-update) | async-done | bytes 33554448 | tf_op jit(solution)/shard_map/all_gather | solution.py:21
  298.3 308.2 %while.12 = (s32[]{:T(128)}, bf16[8,4,256,256]{3,2,1,0:T(8,128)(2,1)}, f32[8]{0:T(128)S(1)}, s32[8]{0:T(128)S(1)}, pred[8]{0:T(512)(128)(4,1)S(1)}, /*index=5*/s...) while((s32[]{:T(128)}, ...), condition=%wide.region_3.4_spmd, body=%wide.region_0.3_spmd.sunk | while | flops 1177093376 | bytes 52828456 | solution.py:56
  300.8 5.1 gather_fusion.1
  305.9 7.4 %convolution_bitcast_fusion.2 = f32[16,2,256,256]{2,3,1,0:T(8,128)} fusion(bf16[16,2,256,256]{3,2,1,0:T(8,128)(2,1)} %gather_fusion.1, bf16[8,16,256,256]{3,2,1,0:T(8,128)(2,1)} %get-tuple-element.271, s32[]{:T(128)S(6)} %select_n.86), kind=kOutput, calls=%fused_computation.5.clone.1 | convolution fusion | flops 1073741824 | bytes 14680068 | tf_op jit(solution)/shard_map/while/body/eval_jaxpr/exy,esyz->esxz/dot_general | solution.py:36
  313.3 10.2 %copy.58 = f32[4,8,256,256]{3,1,2,0:T(8,128)} copy(f32[4,8,256,256]{2,3,1,0:T(8,128)} %bitcast.106) | data formatting | bytes 16777216 | tf_op jit(solution)/shard_map/while
  324.4 6.1 fusion.45
  330.6 1.0 dynamic-slice_bitcast_fusion.2
  332.2 1.8 select_reduce_fusion.2
  334.0 0.9 copy_dynamic-update-slice_fusion.2
  339.3 4.9 gather_fusion.1
  344.2 7.4 %convolution_bitcast_fusion.2 = f32[16,2,256,256]{2,3,1,0:T(8,128)} fusion(bf16[16,2,256,256]{3,2,1,0:T(8,128)(2,1)} %gather_fusion.1, bf16[8,16,256,256]{3,2,1,0:T(8,128)(2,1)} %get-tuple-element.271, s32[]{:T(128)S(6)} %select_n.86), kind=kOutput, calls=%fused_computation.5.clone.1 | convolution fusion | flops 1073741824 | bytes 14680068 | tf_op jit(solution)/shard_map/while/body/eval_jaxpr/exy,esyz->esxz/dot_general | solution.py:36
  351.6 10.2 %copy.58 = f32[4,8,256,256]{3,1,2,0:T(8,128)} copy(f32[4,8,256,256]{2,3,1,0:T(8,128)} %bitcast.106) | data formatting | bytes 16777216 | tf_op jit(solution)/shard_map/while
  362.7 6.1 fusion.45
  368.9 1.0 dynamic-slice_bitcast_fusion.2
  370.5 1.8 select_reduce_fusion.2
  372.3 0.9 copy_dynamic-update-slice_fusion.2
  374.4 0.7 dynamic_update_slice.12
  377.6 4.9 gather_fusion.1
  382.5 7.4 %convolution_bitcast_fusion.2 = f32[16,2,256,256]{2,3,1,0:T(8,128)} fusion(bf16[16,2,256,256]{3,2,1,0:T(8,128)(2,1)} %gather_fusion.1, bf16[8,16,256,256]{3,2,1,0:T(8,128)(2,1)} %get-tuple-element.271, s32[]{:T(128)S(6)} %select_n.86), kind=kOutput, calls=%fused_computation.5.clone.1 | convolution fusion | flops 1073741824 | bytes 14680068 | tf_op jit(solution)/shard_map/while/body/eval_jaxpr/exy,esyz->esxz/dot_general | solution.py:36
  389.9 10.2 %copy.58 = f32[4,8,256,256]{3,1,2,0:T(8,128)} copy(f32[4,8,256,256]{2,3,1,0:T(8,128)} %bitcast.106) | data formatting | bytes 16777216 | tf_op jit(solution)/shard_map/while
  401.1 6.1 fusion.45
  407.2 1.0 dynamic-slice_bitcast_fusion.2
  408.8 1.8 select_reduce_fusion.2
  410.6 0.9 copy_dynamic-update-slice_fusion.2
  415.9 4.9 gather_fusion.1
  420.8 7.4 %convolution_bitcast_fusion.2 = f32[16,2,256,256]{2,3,1,0:T(8,128)} fusion(bf16[16,2,256,256]{3,2,1,0:T(8,128)(2,1)} %gather_fusion.1, bf16[8,16,256,256]{3,2,1,0:T(8,128)(2,1)} %get-tuple-element.271, s32[]{:T(128)S(6)} %select_n.86), kind=kOutput, calls=%fused_computation.5.clone.1 | convolution fusion | flops 1073741824 | bytes 14680068 | tf_op jit(solution)/shard_map/while/body/eval_jaxpr/exy,esyz->esxz/dot_general | solution.py:36
  428.3 10.2 %copy.58 = f32[4,8,256,256]{3,1,2,0:T(8,128)} copy(f32[4,8,256,256]{2,3,1,0:T(8,128)} %bitcast.106) | data formatting | bytes 16777216 | tf_op jit(solution)/shard_map/while
  439.4 6.1 fusion.45
  445.5 1.0 dynamic-slice_bitcast_fusion.2
  447.1 1.8 select_reduce_fusion.2
  448.9 0.9 copy_dynamic-update-slice_fusion.2
  454.3 4.9 gather_fusion.1
  459.2 7.4 %convolution_bitcast_fusion.2 = f32[16,2,256,256]{2,3,1,0:T(8,128)} fusion(bf16[16,2,256,256]{3,2,1,0:T(8,128)(2,1)} %gather_fusion.1, bf16[8,16,256,256]{3,2,1,0:T(8,128)(2,1)} %get-tuple-element.271, s32[]{:T(128)S(6)} %select_n.86), kind=kOutput, calls=%fused_computation.5.clone.1 | convolution fusion | flops 1073741824 | bytes 14680068 | tf_op jit(solution)/shard_map/while/body/eval_jaxpr/exy,esyz->esxz/dot_general | solution.py:36
  466.6 10.2 %copy.58 = f32[4,8,256,256]{3,1,2,0:T(8,128)} copy(f32[4,8,256,256]{2,3,1,0:T(8,128)} %bitcast.106) | data formatting | bytes 16777216 | tf_op jit(solution)/shard_map/while
  477.7 6.1 fusion.45
  483.9 1.0 dynamic-slice_bitcast_fusion.2
  485.5 1.8 select_reduce_fusion.2
  487.3 0.9 copy_dynamic-update-slice_fusion.2
  492.6 5.6 gather_fusion.1
  498.3 7.4 %convolution_bitcast_fusion.2 = f32[16,2,256,256]{2,3,1,0:T(8,128)} fusion(bf16[16,2,256,256]{3,2,1,0:T(8,128)(2,1)} %gather_fusion.1, bf16[8,16,256,256]{3,2,1,0:T(8,128)(2,1)} %get-tuple-element.271, s32[]{:T(128)S(6)} %select_n.86), kind=kOutput, calls=%fused_computation.5.clone.1 | convolution fusion | flops 1073741824 | bytes 14680068 | tf_op jit(solution)/shard_map/while/body/eval_jaxpr/exy,esyz->esxz/dot_general | solution.py:36
  505.7 10.2 %copy.58 = f32[4,8,256,256]{3,1,2,0:T(8,128)} copy(f32[4,8,256,256]{2,3,1,0:T(8,128)} %bitcast.106) | data formatting | bytes 16777216 | tf_op jit(solution)/shard_map/while
  516.8 6.1 fusion.45
  523.0 1.0 dynamic-slice_bitcast_fusion.2
  524.6 1.8 select_reduce_fusion.2
  526.4 0.9 copy_dynamic-update-slice_fusion.2
  531.7 5.3 gather_fusion.1
  537.1 7.4 %convolution_bitcast_fusion.2 = f32[16,2,256,256]{2,3,1,0:T(8,128)} fusion(bf16[16,2,256,256]{3,2,1,0:T(8,128)(2,1)} %gather_fusion.1, bf16[8,16,256,256]{3,2,1,0:T(8,128)(2,1)} %get-tuple-element.271, s32[]{:T(128)S(6)} %select_n.86), kind=kOutput, calls=%fused_computation.5.clone.1 | convolution fusion | flops 1073741824 | bytes 14680068 | tf_op jit(solution)/shard_map/while/body/eval_jaxpr/exy,esyz->esxz/dot_general | solution.py:36
  544.5 10.2 %copy.58 = f32[4,8,256,256]{3,1,2,0:T(8,128)} copy(f32[4,8,256,256]{2,3,1,0:T(8,128)} %bitcast.106) | data formatting | bytes 16777216 | tf_op jit(solution)/shard_map/while
  555.6 6.1 fusion.45
  561.7 1.0 dynamic-slice_bitcast_fusion.2
  563.4 1.8 select_reduce_fusion.2
  565.2 0.9 copy_dynamic-update-slice_fusion.2
  570.5 5.0 gather_fusion.1
  575.5 7.4 %convolution_bitcast_fusion.2 = f32[16,2,256,256]{2,3,1,0:T(8,128)} fusion(bf16[16,2,256,256]{3,2,1,0:T(8,128)(2,1)} %gather_fusion.1, bf16[8,16,256,256]{3,2,1,0:T(8,128)(2,1)} %get-tuple-element.271, s32[]{:T(128)S(6)} %select_n.86), kind=kOutput, calls=%fused_computation.5.clone.1 | convolution fusion | flops 1073741824 | bytes 14680068 | tf_op jit(solution)/shard_map/while/body/eval_jaxpr/exy,esyz->esxz/dot_general | solution.py:36
  583.0 10.2 %copy.58 = f32[4,8,256,256]{3,1,2,0:T(8,128)} copy(f32[4,8,256,256]{2,3,1,0:T(8,128)} %bitcast.106) | data formatting | bytes 16777216 | tf_op jit(solution)/shard_map/while
  594.1 6.1 fusion.45
  600.2 1.0 dynamic-slice_bitcast_fusion.2
  601.8 1.8 select_reduce_fusion.2
  603.6 0.9 copy_dynamic-update-slice_fusion.2
  607.1 64.3 %psum.7 = f32[1]{0:T(128)} all-reduce(f32[1]{0:T(128)} %bitcast.24), channel_id=1, replica_groups=mesh['row'=16,'col'=8] {'row','col'}, use_global_device_ids=true, to_apply=%region_5.6 | all-reduce | flops 1 | bytes 8 | tf_op jit(solution)/shard_map/psum | solution.py:57
  (140 shorter events, 29.5 us)
Async XLA Ops:
  7.2 91.7 %all-gather.7.cloned.1.call-start = ((), (), s32[]{:S(2)}) async-start(), calls=%async_computation.1 | async-start | bytes 18874368 | tf_op jit(solution)/shard_map/all_gather | solution.py:17
  8.0 4.0 copy-start
  8.0 39.8 %copy-start.1 = (s32[8,4]{0,1:T(4,128)S(1)}, s32[8,4]{0,1:T(4,128)}, u32[]{:S(2)}) copy-start(s32[8,4]{0,1:T(4,128)} %param.8) | copy-start | bytes 388
  8.0 39.9 %copy-start.2 = (s32[8]{0:T(128)S(1)}, s32[8]{0:T(128)}, u32[]{:S(2)}) copy-start(s32[8]{0:T(128)} %param.9) | copy-start | bytes 100
  11.2 287.1 %all-gather.5.cloned.1.call-start = ((), (), s32[]{:S(2)}) async-start(), calls=%async_computation | async-start | bytes 35651584 | tf_op jit(solution)/shard_map/all_gather | solution.py:21
Sparse Core Ops, SparseCore 0:
  11.3 87.5 all-gather.6
  101.0 197.2 all-gather.4
where the time goes:
time: 683 us; the launch traced here: 678 us
  waiting for transfers between devices  251 us (37%)
  local copies, waits for them, and re-layouts  160 us (23%)
  matrix products  123 us (18%)
  blocking collectives  99.8 us (15%)
  loops' own time  20.5 us (3%)
  between operations  14.1 us (2%)
  other arithmetic  10 us (1%)
    all_gather x1, waiting for transfers between devices, per_device(): lax.all_gather(cleared, 'row', axis=0, tiled=True)  199 us
    while x16, local copies, waits for them, and re-layouts  89.7 us
    psum x1, blocking collectives, per_device(): trace_total = lax.psum(jnp.sum(parts), ('row', 'col'))  64.3 us
    dot_general x8, matrix products, one_row(): jnp.einsum('exy,esyz->esxz', lhs, fetched, preferred_element_type=jnp.flo...  59.5 us
    all_gather x1, waiting for transfers between devices, per_device(): lax.all_gather(cleared, 'col', axis=1, tiled=True)  51 us
    dot_general x8, matrix products, one_row(): jnp.dot(match, products.reshape(width, block * block), precision=lax.Prec...  49 us
    gather x8, local copies, waits for them, and re-layouts, fetch(): fetched = right_blocks[source_rows]  40.6 us
    all_gather x1, blocking collectives, per_device(): lax.all_gather(x_cols, 'row', axis=0, tiled=True)  23.4 us
  transfers between devices with their start and end apart: 2, of which 2 were waited for; matrix products, arithmetic and copies ran while one was open for 0% of the time, Pallas kernels for 0%

commit v1 on v0

v1 whole, which is shorter than its diff:
```python
import jax
import jax.numpy as jnp
from jax import lax
from jax.experimental import pallas as pl
from jax.experimental.pallas import tpu as pltpu
from jax.sharding import PartitionSpec as P

MESH = pl.DeviceIdType.MESH
BLK = 256
ROWS = 8
SLOTS = 2
KEPT = 4
PACKED = 13
TILE = PACKED * BLK
CUT = TILE // 4
RING = 4
SPAN = 16
LANES = 128
TRACE_LANE = 32
LOOKAHEAD = 1.0


def build_plan():
    items = {}
    step = {"x+": (1, 0), "x-": (-1, 0), "y+": (0, 1), "y-": (0, -1)}

    for q in range(4):
        first, second = ("x", "y") if q < 2 else ("y", "x")
        arrived = {(0, 0): None}

        def send(link, off):
            key = ("B", link, off[0] % RING, off[1] % RING, q)
            pre = arrived[(off[0] % RING, off[1] % RING)]
            items[key] = dict(link=link, size=1.0, pre=[pre] if pre else [])
            move = step[link]
            arrived[((off[0] - move[0]) % RING, (off[1] - move[1]) % RING)] = key

        def line(axis, base):
            unit = (1, 0) if axis == "x" else (0, 1)
            send(axis + "+", base)
            send(axis + "-", base)
            if q % 2 == 0:
                send(axis + "+", (base[0] - unit[0], base[1] - unit[1]))
            else:
                send(axis + "-", (base[0] + unit[0], base[1] + unit[1]))

        line(first, (0, 0))
        for off in range(RING):
            line(second, (off, 0) if first == "x" else (0, off))

    for q in range(4):
        items[("A", "z+", 0, q)] = dict(link="z+", size=1.0, pre=[])
        items[("A", "z-", 0, q)] = dict(link="z-", size=1.0, pre=[])
        if q % 2 == 0:
            items[("A", "z+", 3, q)] = dict(link="z+", size=1.0, pre=[("A", "z+", 0, q)])
            far = ("A", "z+", 3, q)
        else:
            items[("A", "z-", 1, q)] = dict(link="z-", size=1.0, pre=[("A", "z-", 0, q)])
            far = ("A", "z-", 1, q)
        items[("A", "s", 0, q)] = dict(link="s", size=0.2, pre=[])
        items[("A", "s", 3, q)] = dict(link="s", size=0.2, pre=[("A", "z+", 0, q)])
        items[("A", "s", 1, q)] = dict(link="s", size=0.2, pre=[("A", "z-", 0, q)])
        items[("A", "s", 2, q)] = dict(link="s", size=0.2, pre=[far])

    before = []
    for axis in "xyz":
        items[("M", axis + "+", 0)] = dict(link=axis + "+", size=0.02, pre=list(before))
        items[("M", axis + "-", 0)] = dict(link=axis + "-", size=0.02, pre=list(before))
        items[("M", axis + "+", 3)] = dict(link=axis + "+", size=0.02, pre=[("M", axis + "+", 0)])
        before = before + [("M", axis + "+", 0), ("M", axis + "-", 0), ("M", axis + "+", 3)]
    items[("M", "s", 0)] = dict(link="s", size=0.02, pre=list(before))

    after = {key: [] for key in items}
    for key, item in items.items():
        for pre in item["pre"]:
            after[pre].append(key)
    rank = {}

    def depth(key):
        if key not in rank:
            rank[key] = items[key]["size"] + max([depth(k) for k in after[key]] or [0.0])
        return rank[key]

    latency = 0.2
    free = {item["link"]: 0.0 for item in items.values()}
    start, landed = {}, {}
    todo = list(items)
    while todo:
        best = None
        for key in todo:
            if any(pre not in landed for pre in items[key]["pre"]):
                continue
            ready = max([landed[pre] for pre in items[key]["pre"]] or [0.0])
            at = max(ready, free[items[key]["link"]])
            small = 0 if key[0] == "M" else 1
            mark = (at, small, -depth(key))
            if best is None or mark < best[0]:
                best = (mark, key, ready, at)
        _, key, ready, at = best
        todo.remove(key)
        start[key] = (max(ready, at - LOOKAHEAD), at, len(start))
        free[items[key]["link"]] = at + items[key]["size"]
        landed[key] = at + items[key]["size"] + latency
    order = sorted(items, key=lambda key: start[key])
    return order, items, max(landed.values())


ORDER, ITEMS, PLAN_SLOTS = build_plan()
NUMBER = {key: index for index, key in enumerate(ORDER)}


def place():
    row = lax.axis_index("row")
    col = lax.axis_index("col")
    return lax.rem(row, RING), row // RING, col // 2, lax.rem(col, 2)


def turn(value, by):
    return lax.rem(value + by % RING, RING)


def pack_kernel(cols, flags, x_ref, ga, gb, meta, buf, source, line, acc, in_sem, out_sem):
    row = lax.axis_index("row")
    col = lax.axis_index("col")
    x, y, z, core = place()
    for t in range(PACKED):
        source[t] = 0
    lane = lax.broadcasted_iota(jnp.int32, (1, LANES), 1)
    count = jnp.int32(0)
    info = jnp.zeros((1, LANES), jnp.float32)
    for s in range(ROWS * SLOTS):
        entry = cols[s // SLOTS, s % SLOTS]
        live = entry >= 0

        @pl.when(live)
        def _(s=s, count=count):
            source[count] = s

        info = jnp.where(lane == s, entry.astype(jnp.float32), info)
        info = jnp.where(lane == 16 + s, count.astype(jnp.float32), info)
        count = count + live.astype(jnp.int32)

    def fetch(t):
        s = source[t]
        return pltpu.make_async_copy(
            x_ref.at[s // SLOTS, lax.rem(s, SLOTS)], buf.at[pl.ds(t * BLK, BLK)], in_sem.at[t]
        )

    for t in range(PACKED):
        fetch(t).start()
    for t in range(PACKED):
        fetch(t).wait()
    outs = [
        pltpu.make_async_copy(buf, gb.at[row], out_sem.at[0]),
        pltpu.make_async_copy(buf, ga.at[col], out_sem.at[1]),
    ]
    for copy in outs:
        copy.start()

    acc[...] = jnp.zeros_like(acc)
    diag = lax.broadcasted_iota(jnp.int32, (BLK, BLK), 0) == lax.broadcasted_iota(
        jnp.int32, (BLK, BLK), 1
    )

    def term(t, carry):
        s = source[t]
        local = s // SLOTS
        flag = flags[local] == 1
        weight = jnp.where(flag, -1.0, 1.0).astype(jnp.float32)
        block = buf[pl.ds(pl.multiple_of(t * BLK, BLK), BLK), :].astype(jnp.float32)
        acc[...] += weight * jnp.sum((block * block).reshape(BLK // 8, 8, BLK), axis=0)

        @pl.when(flag & (cols[local, lax.rem(s, SLOTS)] == row * ROWS + local))
        def _():
            kept = jnp.where(diag, block, 0.0)
            acc[...] += 2.0 * jnp.sum(kept.reshape(BLK // 8, 8, BLK), axis=0)

        return carry

    lax.fori_loop(0, count, term, 0)
    line[...] = jnp.where(lane == TRACE_LANE, jnp.sum(acc[...]), info)
    last = pltpu.make_async_copy(line, meta.at[core * 64 + z * 16 + y * 4 + x], out_sem.at[2])
    last.start()
    for copy in outs + [last]:
        copy.wait()


def gather_kernel(ga_in, gb_in, meta_in, ga, gb, meta, send_sem, recv_sem):
    x, y, z, core = place()

    def peer(link):
        by = 1 if link.endswith("+") else -1
        if link[0] == "x":
            return {"row": y * RING + turn(x, by), "col": z * 2 + core}
        if link[0] == "y":
            return {"row": turn(y, by) * RING + x, "col": z * 2 + core}
        if link[0] == "z":
            return {"row": y * RING + x, "col": turn(z, by) * 2 + core}
        return {"row": y * RING + x, "col": z * 2 + 1 - core}

    def region(key, at):
        px, py, pz, pcore = at
        if key[0] == "B":
            slot = turn(py, key[3]) * RING + turn(px, key[2])
            return gb.at[slot, pl.ds(key[4] * CUT, CUT)]
        if key[0] == "A":
            slot = turn(pz, key[2]) * 2 + pcore
            return ga.at[slot, pl.ds(key[3] * CUT, CUT)]
        axis = key[1][0]
        if axis == "x":
            return meta.at[pl.ds(pcore * 64 + pz * 16 + py * 4 + turn(px, key[2]), 1)]
        if axis == "y":
            return meta.at[pl.ds(pcore * 64 + pz * 16 + turn(py, key[2]) * 4, 4)]
        if axis == "z":
            return meta.at[pl.ds(pcore * 64 + turn(pz, key[2]) * 16, 16)]
        return meta.at[pl.ds(pcore * 64, 64)]

    def outgoing(key):
        piece = region(key, (x, y, z, core))
        n = NUMBER[key]
        return pltpu.make_async_remote_copy(
            src_ref=piece,
            dst_ref=piece,
            send_sem=send_sem.at[n],
            recv_sem=recv_sem.at[n],
            device_id=peer(key[1]),
            device_id_type=MESH,
        )

    def incoming(key):
        link = key[1]
        by = -1 if link.endswith("+") else 1
        at = (x, y, z, core)
        if link[0] == "x":
            at = (turn(x, by), y, z, core)
        elif link[0] == "y":
            at = (x, turn(y, by), z, core)
        elif link[0] == "z":
            at = (x, y, turn(z, by), core)
        else:
            at = (x, y, z, 1 - core)
        piece = region(key, at)
        n = NUMBER[key]
        return pltpu.make_async_remote_copy(
            src_ref=piece,
            dst_ref=piece,
            send_sem=send_sem.at[n],
            recv_sem=recv_sem.at[n],
            device_id=peer(link),
            device_id_type=MESH,
        )

    barrier = pltpu.get_barrier_semaphore()
    links = ("x+", "x-", "y+", "y-", "z+", "z-", "s")
    for link in links:
        pl.semaphore_signal(barrier, inc=1, device_id=peer(link), device_id_type=MESH)
    pl.semaphore_wait(barrier, len(links))

    seen = set()
    for key in ORDER:
        for pre in ITEMS[key]["pre"]:
            if pre not in seen:
                incoming(pre).wait_recv()
                seen.add(pre)
        outgoing(key).start()
    for key in ORDER:
        if key not in seen:
            incoming(key).wait_recv()
    for key in ORDER:
        outgoing(key).wait_send()


def product_kernel(
    meta, kept, cols, flags, meta_v, x_ref, ga, gb,
    out_ref, trace_ref,
    abuf, bbuf, acc, inv, list_a, list_p, counts, sem,
):
    i = pl.program_id(0)
    x, y, z, core = place()
    row = y * RING + x
    base = (z * 2 + core) * SPAN

    def number(m, at):
        return meta[m, 0, at].astype(jnp.int32)

    def copy_a(slot, n, tile, pos):
        return pltpu.make_async_copy(
            ga.at[tile, pl.ds(pl.multiple_of(pos * BLK, BLK), BLK)], abuf.at[slot, n], sem.at[slot]
        )

    def copy_b(slot, n, tile, pos):
        return pltpu.make_async_copy(
            gb.at[tile, pl.ds(pl.multiple_of(pos * BLK, BLK), BLK)], bbuf.at[slot, n], sem.at[slot]
        )

    def prepare(local, slot):
        for t in range(SPAN):
            inv[t] = -1
        for p in range(KEPT):
            inv[kept[local, p] - base] = p

        def entry(e, carry):
            na, nb = carry
            tile = e // SLOTS
            m = lax.rem(tile, 2) * 64 + tile // 2 * 16 + row
            at = local * SLOTS + lax.rem(e, SLOTS)
            k = number(m, at)

            def live():
                other = k // ROWS
                mb = core * 64 + z * 16 + other
                found = nb
                for s in range(SLOTS):
                    spot = lax.rem(k, ROWS) * SLOTS + s
                    j = number(mb, spot)
                    p = jnp.where(j >= 0, inv[jnp.maximum(j - base, 0)], -1)
                    hit = p >= 0

                    @pl.when(hit)
                    def _(found=found, p=p, spot=spot):
                        list_a[slot, found] = na
                        list_p[slot, found] = p
                        copy_b(slot, found, other, number(mb, 16 + spot)).start()

                    found = found + hit.astype(jnp.int32)

                @pl.when(found > nb)
                def _():
                    copy_a(slot, na, tile, number(m, 16 + at)).start()

                return na + (found > nb).astype(jnp.int32), found

            return lax.cond(k >= 0, live, lambda: (na, nb))

        na, nb = lax.fori_loop(0, 16, entry, (jnp.int32(0), jnp.int32(0)))
        counts[slot, 0] = na
        counts[slot, 1] = nb

    slot = lax.rem(i, 2)

    @pl.when(i == 0)
    def _():
        prepare(0, 0)
        lane = lax.broadcasted_iota(jnp.int32, (128, 1, LANES), 2)
        trace_ref[0, 0] = jnp.sum(jnp.where(lane == TRACE_LANE, meta_v[...], 0.0))

    @pl.when(i + 1 < ROWS)
    def _():
        prepare(i + 1, 1 - slot)

    na, nb = counts[slot, 0], counts[slot, 1]

    def drain(_, carry):
        copy_a(slot, 0, 0, 0).wait()
        return carry

    lax.fori_loop(0, na + nb, drain, 0)
    acc[...] = jnp.zeros_like(acc)

    def product(n, carry):
        p = list_p[slot, n]
        acc[p] += jnp.dot(
            abuf[slot, list_a[slot, n]], bbuf[slot, n], preferred_element_type=jnp.float32
        )
        return carry

    lax.fori_loop(0, nb, product, 0)
    flag = flags[i] == 1
    sign = jnp.where(flag, -1.0, 1.0).astype(jnp.float32)
    for p in range(KEPT):
        j = kept[i, p]
        second = cols[i, 1] == j
        there = second | (cols[i, 0] == j)
        scale = jnp.where(flag & there, 2.0, 0.0).astype(jnp.float32)
        own = x_ref[0, second.astype(jnp.int32)].astype(jnp.float32)
        out_ref[0, p] = (scale * own + sign * acc[p]).astype(jnp.bfloat16)


def per_device(x_blocks, x_cols, out_cols, branch_flag):
    anywhere = pl.BlockSpec(memory_space=pl.ANY)
    scalars = pl.BlockSpec(memory_space=pltpu.SMEM)
    shapes = (
        jax.ShapeDtypeStruct((8, TILE, BLK), jnp.bfloat16),
        jax.ShapeDtypeStruct((16, TILE, BLK), jnp.bfloat16),
        jax.ShapeDtypeStruct((128, 1, LANES), jnp.float32),
    )
    ga, gb, meta = pl.pallas_call(
        pack_kernel,
        name="pack",
        out_shape=shapes,
        in_specs=[scalars, scalars, anywhere],
        out_specs=[anywhere] * 3,
        scratch_shapes=[
            pltpu.VMEM((TILE, BLK), jnp.bfloat16),
            pltpu.SMEM((16,), jnp.int32),
            pltpu.VMEM((1, LANES), jnp.float32),
            pltpu.VMEM((8, BLK), jnp.float32),
            pltpu.SemaphoreType.DMA((PACKED,)),
            pltpu.SemaphoreType.DMA((3,)),
        ],
    )(x_cols, branch_flag, x_blocks)
    ga, gb, meta = pl.pallas_call(
        gather_kernel,
        name="gather",
        out_shape=shapes,
        in_specs=[anywhere] * 3,
        out_specs=[anywhere] * 3,
        scratch_shapes=[
            pltpu.SemaphoreType.DMA((len(ORDER),)),
            pltpu.SemaphoreType.DMA((len(ORDER),)),
        ],
        input_output_aliases={0: 0, 1: 1, 2: 2},
        compiler_params=pltpu.CompilerParams(collective_id=0, has_side_effects=True),
    )(ga, gb, meta)
    purified, trace = pl.pallas_call(
        product_kernel,
        name="product",
        grid=(ROWS,),
        out_shape=(
            jax.ShapeDtypeStruct((ROWS, KEPT, BLK, BLK), jnp.bfloat16),
            jax.ShapeDtypeStruct((1, 1), jnp.float32),
        ),
        in_specs=[
            scalars, scalars, scalars, scalars,
            pl.BlockSpec((128, 1, LANES), lambda i: (0, 0, 0)),
            pl.BlockSpec((1, SLOTS, BLK, BLK), lambda i: (i, 0, 0, 0)),
            anywhere, anywhere,
        ],
        out_specs=[pl.BlockSpec((1, KEPT, BLK, BLK), lambda i: (i, 0, 0, 0)), scalars],
        scratch_shapes=[
            pltpu.VMEM((2, 16, BLK, BLK), jnp.bfloat16),
            pltpu.VMEM((2, 32, BLK, BLK), jnp.bfloat16),
            pltpu.VMEM((KEPT, BLK, BLK), jnp.float32),
            pltpu.SMEM((SPAN,), jnp.int32),
            pltpu.SMEM((2, 32), jnp.int32),
            pltpu.SMEM((2, 32), jnp.int32),
            pltpu.SMEM((2, 2), jnp.int32),
            pltpu.SemaphoreType.DMA((2,)),
        ],
    )(meta, out_cols, x_cols, branch_flag, meta, x_blocks, ga, gb)
    return purified, trace.reshape(1)


def solution(mesh):
    in_specs = (P("row", "col", None, None), P("row", "col"), P("row", "col"), P("row"))
    out_specs = (P("row", "col", None, None), P())
    return jax.shard_map(
        per_device, mesh=mesh, in_specs=in_specs, out_specs=out_specs, check_vma=False
    )
```

time: 683 us -> 191 us (0.28)
  waiting for transfers between devices: 251 us -> 0 us
  Pallas kernels: 0 us -> 186 us
  local copies, waits for them, and re-layouts: 160 us -> 2.02 us
  matrix products: 123 us -> 0 us
  blocking collectives: 99.8 us -> 0 us
  loops' own time: 20.5 us -> 0 us
  between operations: 14.1 us -> 0.66 us
  other arithmetic: 10 us -> 0 us
    all_gather x2 -> x0, waiting for transfers between devices: 250 us -> none  [the longest x1 199 us: per_device(): lax.all_gather(cleared, 'row', axis=0, tiled=True)]
    pallas_call x0 -> x3, Pallas kernels: none -> 186 us  [the longest x1 147 us: per_device(): pl.pallas_call(gather_kernel, name='gather', out_shape=shapes, in_specs=[...]
    dot_general x24 -> x0, matrix products: 123 us -> none  [the longest x8 59.5 us: one_row(): jnp.einsum('exy,esyz->esxz', lhs, fetched, preferred_element_type=jnp.flo...]
    while x20 -> x0, local copies, waits for them, and re-layouts: 90.1 us -> none
    psum x1 -> x0, blocking collectives: 64.3 us -> none  [per_device(): trace_total = lax.psum(jnp.sum(parts), ('row', 'col'))]
    gather x24 -> x0, local copies, waits for them, and re-layouts: 45.7 us -> none  [the longest x8 40.6 us: fetch(): fetched = right_blocks[source_rows]]
    all_gather x2 -> x0, blocking collectives: 35.5 us -> none  [the longest x1 23.4 us: per_device(): lax.all_gather(x_cols, 'row', axis=0, tiled=True)]
    another operation x1 -> x0, loops' own time: 20.5 us -> none  [per_device(): purified, parts = lax.map(one_row, jnp.arange(rows, dtype=jnp.int32))]
  transfers between devices with their start and end apart: 2 -> 0, of which waited for: 2 -> 0; matrix products, arithmetic and copies ran while one was open for 0% -> 0% of each run, Pallas kernels for 0% -> 0%
where the time goes in v1:
time: 191 us; the launch traced here: 189 us
  Pallas kernels  186 us (97%)
  local copies, waits for them, and re-layouts  2.02 us (1%)
    pallas_call x1, Pallas kernels, per_device(): pl.pallas_call(gather_kernel, name='gather', out_shape=shapes, in_specs=[...  147 us
    pallas_call x1, Pallas kernels, per_device(): pl.pallas_call(product_kernel, name='product', grid=(ROWS,), out_shape=(j...  35.3 us
    pallas_call x1, Pallas kernels, per_device(): pl.pallas_call(pack_kernel, name='pack', out_shape=shapes, in_specs=[scal...  4.15 us

profile of v1, /device:TPU:2, one launch (start us, length us, event | category | flops | bytes accessed | tf_op | source)
XLA Modules:
  0.0 189.0 jit_solution(774454083881201575)
XLA Ops:
  0.6 1.3 copy.9.cols
  2.0 4.2 %pack.1 = (bf16[8,3328,256]{2,1,0:T(8,128)(2,1)}, bf16[16,3328,256]{2,1,0:T(8,128)(2,1)}, f32[128,1,128]{2,1,0:T(1,128)}) custom-call(s32[8,2]{1,0:T(8,128)} %copy.9.cols, s32[8]{0:T(128)} %flags.3, bf16[8,2,256,256]{3,2,1,0:T(8,128)(2,1)} %x_ref.3), custom_call_target="tpu_custom_call" | custom-call | tf_op jit(solution)/shard_map/pack/pallas_call | solution.py:387
  6.1 0.0 copy-start
  6.1 146.9 %gather.1 = (bf16[8,3328,256]{2,1,0:T(8,128)(2,1)}, bf16[16,3328,256]{2,1,0:T(8,128)(2,1)}, f32[128,1,128]{2,1,0:T(1,128)}) custom-call(bf16[8,3328,256]{2,1,0:T(8,128)(2,1)} %get-tuple-element.10.ga_in, bf16[16,3328,256]{2,1,0:T(8,128)(2,1)} %get-tuple-element.11.gb_in, ...), custom_call_target="tpu_custom_call", output_to_operand_aliasing={{0}: (0, {}), {1}: (1, {}), {2}: (2, {})} | custom-call | tf_op jit(solution)/shard_map/gather/pallas_call | solution.py:402
  153.0 0.0 copy-done
  153.0 0.7 copy.10.kept
  153.7 35.3 %product.1 = (bf16[8,4,256,256]{3,2,1,0:T(8,128)(2,1)}, f32[1,1]{1,0:T(1,128)}) custom-call(f32[128,1,128]{2,1,0:T(1,128)} %get-tuple-element.13.meta.meta_v, s32[8,4]{1,0:T(8,128)} %copy.10.kept, s32[8,2]{1,0:T(8,128)} %copy.9.cols, s32[8]{0:T(128)} %flags.3, f32[128,1,128]{2,1,0:T(1,128)} %get-tuple-element.13.meta.meta_v, bf16[8,2,256,256]{3,2,1,0:T(8,128)(2,1)} %x_ref.3, ...), custom_call_target="tpu_custom_call" | custom-call | tf_op jit(solution)/shard_map/product/pallas_call | solution.py:415
Async XLA Ops:
  6.1 146.9 %copy-start = (s32[8,4]{0,1:T(4,128)S(1)}, s32[8,4]{0,1:T(4,128)}, u32[]{:S(2)}) copy-start(s32[8,4]{0,1:T(4,128)} %param.6) | copy-start | bytes 388

commit v2 on v1

v2 whole, which is shorter than its diff:
```python
import jax
import jax.numpy as jnp
from jax import lax
from jax.experimental import pallas as pl
from jax.experimental.pallas import tpu as pltpu
from jax.sharding import PartitionSpec as P

MESH = pl.DeviceIdType.MESH
BLK = 256
ROWS = 8
SLOTS = 2
KEPT = 4
PACKED = 13
PART = 64
PER = BLK // PART
TILE = PACKED * PER
CUT = TILE // 4
RING = 4
SPAN = 16
LANES = 128
LOOKAHEAD = 1.0


def build_plan():
    items = {}
    step = {"x+": (1, 0), "x-": (-1, 0), "y+": (0, 1), "y-": (0, -1)}

    for q in range(4):
        first, second = ("x", "y") if q < 2 else ("y", "x")
        arrived = {(0, 0): None}

        def send(link, off):
            key = ("B", link, off[0] % RING, off[1] % RING, q)
            pre = arrived[(off[0] % RING, off[1] % RING)]
            items[key] = dict(link=link, size=1.0, pre=[pre] if pre else [])
            move = step[link]
            arrived[((off[0] - move[0]) % RING, (off[1] - move[1]) % RING)] = key

        def line(axis, base):
            unit = (1, 0) if axis == "x" else (0, 1)
            send(axis + "+", base)
            send(axis + "-", base)
            if q % 2 == 0:
                send(axis + "+", (base[0] - unit[0], base[1] - unit[1]))
            else:
                send(axis + "-", (base[0] + unit[0], base[1] + unit[1]))

        line(first, (0, 0))
        for off in range(RING):
            line(second, (off, 0) if first == "x" else (0, off))

    for q in range(4):
        items[("A", "z+", 0, q)] = dict(link="z+", size=1.0, pre=[])
        items[("A", "z-", 0, q)] = dict(link="z-", size=1.0, pre=[])
        if q % 2 == 0:
            items[("A", "z+", 3, q)] = dict(link="z+", size=1.0, pre=[("A", "z+", 0, q)])
            far = ("A", "z+", 3, q)
        else:
            items[("A", "z-", 1, q)] = dict(link="z-", size=1.0, pre=[("A", "z-", 0, q)])
            far = ("A", "z-", 1, q)
        items[("A", "s", 0, q)] = dict(link="s", size=0.2, pre=[])
        items[("A", "s", 3, q)] = dict(link="s", size=0.2, pre=[("A", "z+", 0, q)])
        items[("A", "s", 1, q)] = dict(link="s", size=0.2, pre=[("A", "z-", 0, q)])
        items[("A", "s", 2, q)] = dict(link="s", size=0.2, pre=[far])

    before = []
    for axis in "xyz":
        items[("M", axis + "+", 0)] = dict(link=axis + "+", size=0.02, pre=list(before))
        items[("M", axis + "-", 0)] = dict(link=axis + "-", size=0.02, pre=list(before))
        items[("M", axis + "+", 3)] = dict(link=axis + "+", size=0.02, pre=[("M", axis + "+", 0)])
        before = before + [("M", axis + "+", 0), ("M", axis + "-", 0), ("M", axis + "+", 3)]
    items[("M", "s", 0)] = dict(link="s", size=0.02, pre=list(before))

    source = {}
    for key in items:
        if key[0] == "B":
            move = step[key[1]]
            source[((key[2] - move[0]) % RING, (key[3] - move[1]) % RING, key[4])] = key

    def group(dx, dy):
        return 2 * LINE_ORDER.index(dy) + (1 if dx == 2 else 0)

    due = {key: float(PAIRS * 2) for key in items}
    for (dx, dy, q), key in source.items():
        due[key] = DEADLINES[group(dx, dy)]
    after = {key: [] for key in items}
    for key, item in items.items():
        for pre in item["pre"]:
            after[pre].append(key)
    rank = {}

    def urgency(key):
        if key not in rank:
            rank[key] = min(
                [due[key]] + [urgency(k) - items[k]["size"] - SLACK for k in after[key]]
            )
        return rank[key]

    free = {item["link"]: 0.0 for item in items.values()}
    start, landed = {}, {}
    todo = list(items)
    while todo:
        best = None
        for key in todo:
            if any(pre not in landed for pre in items[key]["pre"]):
                continue
            ready = max([landed[pre] + SLACK for pre in items[key]["pre"]] or [0.0])
            at = max(ready, free[items[key]["link"]])
            small = 0 if key[0] == "M" else 1
            mark = (at, small, urgency(key))
            if best is None or mark < best[0]:
                best = (mark, key, ready, at)
        _, key, ready, at = best
        todo.remove(key)
        start[key] = (max(ready, at - LOOKAHEAD), at, len(start))
        free[items[key]["link"]] = at + items[key]["size"]
        landed[key] = at + items[key]["size"]
    events = [(start[key], ("send", key)) for key in items]

    clock = max(landed[key] for key in items if key[0] == "A") + 0.2
    events.append(((clock, 0.0, 0), ("rows", None)))
    needs = []
    for n in range(PAIRS - LEFT):
        need = [key for (dx, dy, q), key in source.items() if group(dx, dy) <= n
                and group(dx, dy) // 2 == n // 2]
        needs.append(need)
        there = max([landed[key] for key in need]) + 0.2
        began = max(clock - (0.4 if n else 0.0), there)
        events.append(((began, 0.5, n), ("load", n)))
        clock = max(clock, began + 0.3)
        for i in range(0, ROWS, GROUP):
            events.append(((clock, 1.0, i), ("work", (n, i))))
            clock = clock + CHUNK * GROUP
    events.sort()
    order = sorted(items, key=lambda key: start[key])
    return [event for _, event in events], order, items, needs, max(landed.values()), clock


PAIRS = 8
LEFT = 1
LINE_ORDER = (0, 1, 3, 2)
DEADLINES = (2.0, 3.0, 6.0, 7.0, 10.0, 11.0, 14.0, 15.0)
SLACK = 1.0
CHUNK = 0.13
GROUP = 4
EVENTS, ORDER, ITEMS, NEEDS, PLAN_SLOTS, PLAN_WORK = build_plan()
NUMBER = {key: index for index, key in enumerate(ORDER)}


def place():
    row = lax.axis_index("row")
    col = lax.axis_index("col")
    return lax.rem(row, RING), row // RING, col // 2, lax.rem(col, 2)


def turn(value, by):
    return lax.rem(value + by % RING, RING)


def pack_kernel(
    cols, flags, x_ref, ga, gb, meta, share, buf, source, line, total, acc, in_sem, out_sem
):
    row = lax.axis_index("row")
    col = lax.axis_index("col")
    x, y, z, core = place()
    for t in range(PACKED):
        source[t] = 0
    lane = lax.broadcasted_iota(jnp.int32, (1, LANES), 1)
    count = jnp.int32(0)
    info = jnp.zeros((1, LANES), jnp.int32)
    for s in range(ROWS * SLOTS):
        entry = cols[s // SLOTS, s % SLOTS]
        live = entry >= 0

        @pl.when(live)
        def _(s=s, count=count):
            source[count] = s

        info = jnp.where(lane == s, entry, info)
        info = jnp.where(lane == 16 + s, jnp.where(live, count, 0), info)
        count = count + live.astype(jnp.int32)

    def fetch(t):
        s = source[t]
        return pltpu.make_async_copy(
            x_ref.at[s // SLOTS, lax.rem(s, SLOTS)], buf.at[pl.ds(t * PER, PER)], in_sem.at[t]
        )

    for t in range(PACKED):
        fetch(t).start()
    line[...] = info
    outs = [
        pltpu.make_async_copy(line, meta.at[col], out_sem.at[2]),
        pltpu.make_async_copy(line, meta.at[8 + row], out_sem.at[3]),
    ]
    for copy in outs:
        copy.start()
    for t in range(PACKED):
        fetch(t).wait()
    outs = outs + [
        pltpu.make_async_copy(buf, gb.at[row], out_sem.at[0]),
        pltpu.make_async_copy(buf, ga.at[col], out_sem.at[1]),
    ]
    for copy in outs[2:]:
        copy.start()

    acc[...] = jnp.zeros_like(acc)
    diag = lax.broadcasted_iota(jnp.int32, (BLK, BLK), 0) == lax.broadcasted_iota(
        jnp.int32, (BLK, BLK), 1
    )

    def term(t, carry):
        s = source[t]
        local = s // SLOTS
        flag = flags[local] == 1
        weight = jnp.where(flag, -1.0, 1.0).astype(jnp.float32)
        block = buf[pl.ds(t * PER, PER)].reshape(BLK, BLK).astype(jnp.float32)
        acc[...] += weight * jnp.sum((block * block).reshape(BLK // 8, 8, BLK), axis=0)

        @pl.when(flag & (cols[local, lax.rem(s, SLOTS)] == row * ROWS + local))
        def _():
            kept = jnp.where(diag, block, 0.0)
            acc[...] += 2.0 * jnp.sum(kept.reshape(BLK // 8, 8, BLK), axis=0)

        return carry

    lax.fori_loop(0, count, term, 0)
    total[...] = jnp.where(lane == 0, jnp.sum(acc[...]), 0.0)
    last = pltpu.make_async_copy(
        total, share.at[core * 64 + z * 16 + y * 4 + x], out_sem.at[4]
    )
    last.start()
    for copy in outs + [last]:
        copy.wait()


def gather_kernel(
    kept, ga_in, gb_in, meta_in, share_in, ga, gb, meta, share, part,
    a0, a1, b0, b1, acc, words, send_sem, recv_sem, note_send, note_recv, load_sem, out_sem,
):
    row = lax.axis_index("row")
    col = lax.axis_index("col")
    x, y, z, core = place()

    def peer(link):
        by = 1 if link.endswith("+") else -1
        if link[0] == "x":
            return {"row": y * RING + turn(x, by), "col": z * 2 + core}
        if link[0] == "y":
            return {"row": turn(y, by) * RING + x, "col": z * 2 + core}
        if link[0] == "z":
            return {"row": y * RING + x, "col": turn(z, by) * 2 + core}
        return {"row": y * RING + x, "col": z * 2 + 1 - core}

    def region(key, at):
        px, py, pz, pcore = at
        if key[0] == "B":
            slot = turn(py, key[3]) * RING + turn(px, key[2])
            return gb.at[slot, pl.ds(key[4] * CUT, CUT)]
        if key[0] == "A":
            slot = turn(pz, key[2]) * 2 + pcore
            return ga.at[slot, pl.ds(key[3] * CUT, CUT)]
        axis = key[1][0]
        if axis == "x":
            return share.at[pl.ds(pcore * 64 + pz * 16 + py * 4 + turn(px, key[2]), 1)]
        if axis == "y":
            return share.at[pl.ds(pcore * 64 + pz * 16 + turn(py, key[2]) * 4, 4)]
        if axis == "z":
            return share.at[pl.ds(pcore * 64 + turn(pz, key[2]) * 16, 16)]
        return share.at[pl.ds(pcore * 64, 64)]

    def outgoing(key):
        piece = region(key, (x, y, z, core))
        n = NUMBER[key]
        return pltpu.make_async_remote_copy(
            src_ref=piece,
            dst_ref=piece,
            send_sem=send_sem.at[n],
            recv_sem=recv_sem.at[n],
            device_id=peer(key[1]),
            device_id_type=MESH,
        )

    def incoming(key):
        link = key[1]
        by = -1 if link.endswith("+") else 1
        at = (x, y, z, core)
        if link[0] == "x":
            at = (turn(x, by), y, z, core)
        elif link[0] == "y":
            at = (x, turn(y, by), z, core)
        elif link[0] == "z":
            at = (x, y, turn(z, by), core)
        else:
            at = (x, y, z, 1 - core)
        piece = region(key, at)
        n = NUMBER[key]
        return pltpu.make_async_remote_copy(
            src_ref=piece,
            dst_ref=piece,
            send_sem=send_sem.at[n],
            recv_sem=recv_sem.at[n],
            device_id=peer(link),
            device_id_type=MESH,
        )

    def note_slots(n):
        if n < 7:
            return col, lax.rem(col + 7 - n, 8)
        return 8 + row, 8 + lax.rem(row + 22 - n, 16)

    def note_device(n):
        if n < 7:
            return {"row": row, "col": lax.rem(col + n + 1, 8)}
        return {"row": lax.rem(row + n - 6, 16), "col": col}

    def note(n, slot):
        return pltpu.make_async_remote_copy(
            src_ref=meta.at[slot],
            dst_ref=meta.at[slot],
            send_sem=note_send.at[n],
            recv_sem=note_recv.at[n],
            device_id=note_device(n),
            device_id_type=MESH,
        )

    barrier = pltpu.get_barrier_semaphore()
    for n in range(22):
        pl.semaphore_signal(barrier, inc=1, device_id=note_device(n), device_id_type=MESH)
    zero = jnp.zeros((PART, BLK), jnp.bfloat16)
    for t in range(PER):
        b0[2 * TILE + t] = zero
        b1[2 * TILE + t] = zero
    pl.semaphore_wait(barrier, 22)
    for n in range(22):
        note(n, note_slots(n)[0]).start()

    def loads(n):
        c = pair_of(n, x, y)
        abuf, bbuf = (a0, b0) if n % 2 == 0 else (a1, b1)
        pieces = (
            (ga.at[c], abuf),
            (gb.at[2 * c], bbuf.at[pl.ds(0, TILE)]),
            (gb.at[2 * c + 1], bbuf.at[pl.ds(TILE, TILE)]),
        )
        return [
            pltpu.make_async_copy(piece, to, load_sem.at[n % 2, t])
            for t, (piece, to) in enumerate(pieces)
        ]

    def whole(ref, index):
        return jnp.concatenate([ref[index * PER + t] for t in range(PER)], axis=0)

    def work(n, i):
        c = pair_of(n, x, y)
        abuf, bbuf = (a0, b0) if n % 2 == 0 else (a1, b1)
        sums = [None] * KEPT
        for e in range(SLOTS):
            k = words[c, 0, i * SLOTS + e]
            pos = words[c, 0, 16 + i * SLOTS + e]
            local = jnp.maximum(k - c * SPAN, 0)
            half = local // ROWS
            spot = (local - half * ROWS) * SLOTS
            line = 8 + 2 * c + half
            first, second = words[line, 0, spot], words[line, 0, spot + 1]
            at_first = words[line, 0, 16 + spot] + half * PACKED
            at_second = words[line, 0, 17 + spot] + half * PACKED
            left = whole(abuf, pos)
            for p in range(KEPT):
                j = jnp.where(k >= 0, kept[i, p], -2)
                index = jnp.where(first == j, at_first, jnp.where(second == j, at_second, 2 * PACKED))
                right = whole(bbuf, index)
                term = jnp.dot(left, right, preferred_element_type=jnp.float32)
                sums[p] = term if sums[p] is None else sums[p] + term
        for p in range(KEPT):
            if n == 0:
                acc[i * KEPT + p] = sums[p]
            else:
                acc[i * KEPT + p] += sums[p]

    def result(i):
        piece = pl.ds(i * KEPT, GROUP * KEPT)
        return pltpu.make_async_copy(acc.at[piece], part.at[piece], out_sem.at[i // GROUP])

    seen = set()

    def await_all(keys):
        for key in keys:
            if key not in seen:
                incoming(key).wait_recv()
                seen.add(key)

    final = PAIRS - LEFT - 1
    for kind, what in EVENTS:
        if kind == "send":
            await_all(ITEMS[what]["pre"])
            outgoing(what).start()
        elif kind == "rows":
            for n in range(22):
                note(n, note_slots(n)[1]).wait_recv()
            words_copy = pltpu.make_async_copy(meta, words, load_sem.at[2, 0])
            words_copy.start()
            await_all([key for key in ORDER if key[0] == "A"])
            words_copy.wait()
        elif kind == "load":
            await_all(NEEDS[what])
            for copy in loads(what):
                copy.start()
        else:
            n, i = what
            if i == 0:
                for copy in loads(n):
                    copy.wait()
            lax.fori_loop(i, i + GROUP, lambda t, carry, n=n: work(n, t), None)
            if n == final:
                result(i).start()
    await_all(ORDER)
    for i in range(0, ROWS, GROUP):
        result(i).wait()
    for key in ORDER:
        outgoing(key).wait_send()
    for n in range(22):
        note(n, note_slots(n)[0]).wait_send()


def pair_of(n, x, y):
    line = turn(y, LINE_ORDER[n // 2])
    half = x // 2 if n % 2 == 0 else 1 - x // 2
    return line * 2 + half


def product_kernel(
    meta, kept, cols, flags, share, part_ref, x_ref, ga, gb,
    out_ref, trace_ref,
    abuf, bbuf, acc, sem,
):
    i = pl.program_id(0)
    x, y, z, core = place()

    def loads(n):
        c = pair_of(PAIRS - LEFT + n, x, y)
        return [
            pltpu.make_async_copy(ga.at[c], abuf.at[n], sem.at[n, 0]),
            pltpu.make_async_copy(gb.at[2 * c], bbuf.at[n, pl.ds(0, TILE)], sem.at[n, 1]),
            pltpu.make_async_copy(gb.at[2 * c + 1], bbuf.at[n, pl.ds(TILE, TILE)], sem.at[n, 2]),
        ]

    @pl.when(i == 0)
    def _():
        for n in range(LEFT):
            for copy in loads(n):
                copy.start()
        lane = lax.broadcasted_iota(jnp.int32, (128, 1, LANES), 2)
        trace_ref[0, 0] = jnp.sum(jnp.where(lane == 0, share[...], 0.0))
        for n in range(LEFT):
            for copy in loads(n):
                copy.wait()

    acc[...] = part_ref[0]
    for n in range(LEFT):
        c = pair_of(PAIRS - LEFT + n, x, y)
        for e in range(SLOTS):
            k = meta[c, 0, i * SLOTS + e]

            @pl.when(k >= 0)
            def _(n=n, c=c, e=e, k=k):
                pos = meta[c, 0, 16 + i * SLOTS + e]
                other = k // ROWS
                for s in range(SLOTS):
                    spot = lax.rem(k, ROWS) * SLOTS + s
                    j = meta[8 + other, 0, spot]
                    p = jnp.int32(-1)
                    for t in range(KEPT):
                        p = jnp.where(kept[i, t] == j, t, p)

                    @pl.when(p >= 0)
                    def _(spot=spot, p=p):
                        at = meta[8 + other, 0, 16 + spot] + (other - 2 * c) * PACKED
                        acc[p] += jnp.dot(
                            abuf[n, pl.ds(pos * PER, PER)].reshape(BLK, BLK),
                            bbuf[n, pl.ds(at * PER, PER)].reshape(BLK, BLK),
                            preferred_element_type=jnp.float32,
                        )

    flag = flags[i] == 1
    sign = jnp.where(flag, -1.0, 1.0).astype(jnp.float32)
    for p in range(KEPT):
        j = kept[i, p]
        second = cols[i, 1] == j
        there = second | (cols[i, 0] == j)
        scale = jnp.where(flag & there, 2.0, 0.0).astype(jnp.float32)
        own = x_ref[0, second.astype(jnp.int32)].astype(jnp.float32)
        out_ref[0, p] = (scale * own + sign * acc[p]).astype(jnp.bfloat16)


def per_device(x_blocks, x_cols, out_cols, branch_flag):
    anywhere = pl.BlockSpec(memory_space=pl.ANY)
    scalars = pl.BlockSpec(memory_space=pltpu.SMEM)
    shapes = (
        jax.ShapeDtypeStruct((8, TILE, PART, BLK), jnp.bfloat16),
        jax.ShapeDtypeStruct((16, TILE, PART, BLK), jnp.bfloat16),
        jax.ShapeDtypeStruct((24, 1, LANES), jnp.int32),
        jax.ShapeDtypeStruct((128, 1, LANES), jnp.float32),
    )
    gathered = pl.pallas_call(
        pack_kernel,
        name="pack",
        out_shape=shapes,
        in_specs=[scalars, scalars, anywhere],
        out_specs=[anywhere] * 4,
        scratch_shapes=[
            pltpu.VMEM((TILE, PART, BLK), jnp.bfloat16),
            pltpu.SMEM((16,), jnp.int32),
            pltpu.VMEM((1, LANES), jnp.int32),
            pltpu.VMEM((1, LANES), jnp.float32),
            pltpu.VMEM((8, BLK), jnp.float32),
            pltpu.SemaphoreType.DMA((PACKED,)),
            pltpu.SemaphoreType.DMA((5,)),
        ],
    )(x_cols, branch_flag, x_blocks.reshape(ROWS, SLOTS, PER, PART, BLK))
    ga, gb, meta, share, part = pl.pallas_call(
        gather_kernel,
        name="gather",
        out_shape=shapes + (jax.ShapeDtypeStruct((ROWS * KEPT, BLK, BLK), jnp.float32),),
        in_specs=[scalars] + [anywhere] * 4,
        out_specs=[anywhere] * 5,
        scratch_shapes=[
            pltpu.VMEM((TILE, PART, BLK), jnp.bfloat16),
            pltpu.VMEM((TILE, PART, BLK), jnp.bfloat16),
            pltpu.VMEM((2 * TILE + PER, PART, BLK), jnp.bfloat16),
            pltpu.VMEM((2 * TILE + PER, PART, BLK), jnp.bfloat16),
            pltpu.VMEM((ROWS * KEPT, BLK, BLK), jnp.float32),
            pltpu.SMEM((24, 1, LANES), jnp.int32),
            pltpu.SemaphoreType.DMA((len(ORDER),)),
            pltpu.SemaphoreType.DMA((len(ORDER),)),
            pltpu.SemaphoreType.DMA((22,)),
            pltpu.SemaphoreType.DMA((22,)),
            pltpu.SemaphoreType.DMA((3, 3)),
            pltpu.SemaphoreType.DMA((ROWS // GROUP,)),
        ],
        input_output_aliases={1: 0, 2: 1, 3: 2, 4: 3},
        compiler_params=pltpu.CompilerParams(collective_id=0, has_side_effects=True),
    )(out_cols, *gathered)
    purified, trace = pl.pallas_call(
        product_kernel,
        name="product",
        grid=(ROWS,),
        out_shape=(
            jax.ShapeDtypeStruct((ROWS, KEPT, BLK, BLK), jnp.bfloat16),
            jax.ShapeDtypeStruct((1, 1), jnp.float32),
        ),
        in_specs=[
            scalars, scalars, scalars, scalars,
            pl.BlockSpec((128, 1, LANES), lambda i: (0, 0, 0)),
            pl.BlockSpec((1, KEPT, BLK, BLK), lambda i: (i, 0, 0, 0)),
            pl.BlockSpec((1, SLOTS, BLK, BLK), lambda i: (i, 0, 0, 0)),
            anywhere, anywhere,
        ],
        out_specs=[pl.BlockSpec((1, KEPT, BLK, BLK), lambda i: (i, 0, 0, 0)), scalars],
        scratch_shapes=[
            pltpu.VMEM((LEFT, TILE, PART, BLK), jnp.bfloat16),
            pltpu.VMEM((LEFT, 2 * TILE, PART, BLK), jnp.bfloat16),
            pltpu.VMEM((KEPT, BLK, BLK), jnp.float32),
            pltpu.SemaphoreType.DMA((LEFT, 3)),
        ],
    )(meta, out_cols, x_cols, branch_flag, share,
      part.reshape(ROWS, KEPT, BLK, BLK), x_blocks, ga, gb)
    return purified, trace.reshape(1)


def solution(mesh):
    in_specs = (P("row", "col", None, None), P("row", "col"), P("row", "col"), P("row"))
    out_specs = (P("row", "col", None, None), P())
    return jax.shard_map(
        per_device, mesh=mesh, in_specs=in_specs, out_specs=out_specs, check_vma=False
    )
```

time: 191 us -> 172 us (0.901)
  Pallas kernels: 186 us -> 168 us
    pallas_call x1, Pallas kernels: 35.3 us -> 13.1 us  [per_device(): pl.pallas_call(product_kernel, name='product', grid=(ROWS,), out_shape=(j...]
    pallas_call x1, Pallas kernels: 147 us -> 151 us  [per_device(): pl.pallas_call(gather_kernel, name='gather', out_shape=shapes + (jax.Shap...]
where the time goes in v2:
time: 172 us; the launch traced here: 171 us
  Pallas kernels  168 us (98%)
  local copies, waits for them, and re-layouts  2.69 us (2%)
    pallas_call x1, Pallas kernels, per_device(): pl.pallas_call(gather_kernel, name='gather', out_shape=shapes + (jax.Shap...  151 us
    pallas_call x1, Pallas kernels, per_device(): pl.pallas_call(product_kernel, name='product', grid=(ROWS,), out_shape=(j...  13.1 us
    pallas_call x1, Pallas kernels, per_device(): pl.pallas_call(pack_kernel, name='pack', out_shape=shapes, in_specs=[scal...  4.14 us

profile of v2, /device:TPU:2, one launch (start us, length us, event | category | flops | bytes accessed | tf_op | source)
XLA Modules:
  0.0 171.2 jit_solution(7259908719844626732)
XLA Ops:
  0.6 1.3 copy.10.cols
  2.0 1.3 copy.11.kept
  3.3 4.1 %pack.1 = (bf16[8,52,64,256]{3,2,1,0:T(8,128)(2,1)}, bf16[16,52,64,256]{3,2,1,0:T(8,128)(2,1)}, s32[24,1,128]{2,1,0:T(1,128)}, f32[128,1,128]{2,1,0:T(1,128)}) custom-call(s32[8,2]{1,0:T(8,128)} %copy.10.cols, s32[8]{0:T(128)} %flags.3, bf16[8,2,4,64,256]{4,3,2,1,0:T(8,128)(2,1)} %bitcast.4), custom_call_target="tpu_custom_call" | custom-call | tf_op jit(solution)/shard_map/pack/pallas_call | solution.py:505
  7.5 150.6 %gather.1 = (bf16[8,52,64,256]{3,2,1,0:T(8,128)(2,1)}, bf16[16,52,64,256]{3,2,1,0:T(8,128)(2,1)}, s32[24,1,128]{2,1,0:T(1,128)}, f32[128,1,128]{2,1,0:T(1,128)}, f32[32,256,256]{2,1,0:T(8,128)}) custom-call(s32[8,4]{1,0:T(8,128)} %copy.11.kept, ...), custom_call_target="tpu_custom_call", output_to_operand_aliasing={{0}: (1, {}), {1}: (2, {}), {2}: (3, {}), {3}: (4, {})} | custom-call | tf_op jit(solution)/shard_map/gather/pallas_call | solution.py:521
  158.1 13.1 %product.1 = (bf16[8,4,256,256]{3,2,1,0:T(8,128)(2,1)}, f32[1,1]{1,0:T(1,128)}) custom-call(s32[24,1,128]{2,1,0:T(1,128)} %get-tuple-element.17.meta, s32[8,4]{1,0:T(8,128)} %copy.11.kept, s32[8,2]{1,0:T(8,128)} %copy.10.cols, s32[8]{0:T(128)} %flags.3, f32[128,1,128]{2,1,0:T(1,128)} %get-tuple-element.18.share, f32[8,4,256,256]{3,2,1,0:T(8,128)} %bitcast.3, ...), custom_call_target="tpu_custom_call" | custom-call | tf_op jit(solution)/shard_map/product/pallas_call | solution.py:544

commit v3 on v2

--- a/solution.py
+++ b/solution.py
@@ -18,7 +18,7 @@
 RING = 4
 SPAN = 16
 LANES = 128
-LOOKAHEAD = 1.0
+LOOKAHEAD = 0.4
 
 
 def build_plan():
@@ -105,6 +105,8 @@
             if any(pre not in landed for pre in items[key]["pre"]):
                 continue
             ready = max([landed[pre] + SLACK for pre in items[key]["pre"]] or [0.0])
+            if key[0] == "M":
+                ready = max(ready, SHARE_AT)
             at = max(ready, free[items[key]["link"]])
             small = 0 if key[0] == "M" else 1
             mark = (at, small, urgency(key))
@@ -116,6 +118,9 @@
         free[items[key]["link"]] = at + items[key]["size"]
         landed[key] = at + items[key]["size"]
     events = [(start[key], ("send", key)) for key in items]
+
+    events.append(((0.4, 0.0, 0), ("trace", None)))
+    events.append(((SHARE_AT - LOOKAHEAD - 0.1, 0.0, 0), ("share", None)))
 
     clock = max(landed[key] for key in items if key[0] == "A") + 0.2
     events.append(((clock, 0.0, 0), ("rows", None)))
@@ -137,10 +142,11 @@
 
 
 PAIRS = 8
+SHARE_AT = 3.0
 LEFT = 1
 LINE_ORDER = (0, 1, 3, 2)
 DEADLINES = (2.0, 3.0, 6.0, 7.0, 10.0, 11.0, 14.0, 15.0)
-SLACK = 1.0
+SLACK = 0.5
 CHUNK = 0.13
 GROUP = 4
 EVENTS, ORDER, ITEMS, NEEDS, PLAN_SLOTS, PLAN_WORK = build_plan()
@@ -157,19 +163,16 @@
     return lax.rem(value + by % RING, RING)
 
 
-def pack_kernel(
-    cols, flags, x_ref, ga, gb, meta, share, buf, source, line, total, acc, in_sem, out_sem
-):
+def pack_kernel(cols, x_ref, ga, gb, meta, buf, source, line, in_sem, out_sem):
     row = lax.axis_index("row")
     col = lax.axis_index("col")
-    x, y, z, core = place()
     for t in range(PACKED):
         source[t] = 0
     lane = lax.broadcasted_iota(jnp.int32, (1, LANES), 1)
     count = jnp.int32(0)
     info = jnp.zeros((1, LANES), jnp.int32)
     for s in range(ROWS * SLOTS):
-        entry = cols[s // SLOTS, s % SLOTS]
+        entry = cols[s % SLOTS, s // SLOTS]
         live = entry >= 0
 
         @pl.when(live)
@@ -181,62 +184,32 @@
         count = count + live.astype(jnp.int32)
 
     def fetch(t):
-        s = source[t]
         return pltpu.make_async_copy(
-            x_ref.at[s // SLOTS, lax.rem(s, SLOTS)], buf.at[pl.ds(t * PER, PER)], in_sem.at[t]
+            x_ref.at[pl.ds(source[t] * PER, PER)], buf.at[pl.ds(t * PER, PER)], in_sem.at[t]
         )
 
     for t in range(PACKED):
         fetch(t).start()
     line[...] = info
-    outs = [
-        pltpu.make_async_copy(line, meta.at[col], out_sem.at[2]),
-        pltpu.make_async_copy(line, meta.at[8 + row], out_sem.at[3]),
-    ]
-    for copy in outs:
-        copy.start()
+    outs = []
     for t in range(PACKED):
         fetch(t).wait()
-    outs = outs + [
-        pltpu.make_async_copy(buf, gb.at[row], out_sem.at[0]),
-        pltpu.make_async_copy(buf, ga.at[col], out_sem.at[1]),
-    ]
-    for copy in outs[2:]:
+        piece = pl.ds(t * PER, PER)
+        for n, to in enumerate((gb.at[row, piece], ga.at[col, piece])):
+            copy = pltpu.make_async_copy(buf.at[piece], to, out_sem.at[2 * t + n])
+            copy.start()
+            outs.append(copy)
+    for n, slot in enumerate((col, 8 + row)):
+        copy = pltpu.make_async_copy(line, meta.at[slot], out_sem.at[2 * PACKED + n])
         copy.start()
-
-    acc[...] = jnp.zeros_like(acc)
-    diag = lax.broadcasted_iota(jnp.int32, (BLK, BLK), 0) == lax.broadcasted_iota(
-        jnp.int32, (BLK, BLK), 1
-    )
-
-    def term(t, carry):
-        s = source[t]
-        local = s // SLOTS
-        flag = flags[local] == 1
-        weight = jnp.where(flag, -1.0, 1.0).astype(jnp.float32)
-        block = buf[pl.ds(t * PER, PER)].reshape(BLK, BLK).astype(jnp.float32)
-        acc[...] += weight * jnp.sum((block * block).reshape(BLK // 8, 8, BLK), axis=0)
-
-        @pl.when(flag & (cols[local, lax.rem(s, SLOTS)] == row * ROWS + local))
-        def _():
-            kept = jnp.where(diag, block, 0.0)
-            acc[...] += 2.0 * jnp.sum(kept.reshape(BLK // 8, 8, BLK), axis=0)
-
-        return carry
-
-    lax.fori_loop(0, count, term, 0)
-    total[...] = jnp.where(lane == 0, jnp.sum(acc[...]), 0.0)
-    last = pltpu.make_async_copy(
-        total, share.at[core * 64 + z * 16 + y * 4 + x], out_sem.at[4]
-    )
-    last.start()
-    for copy in outs + [last]:
+        outs.append(copy)
+    for copy in outs:
         copy.wait()
 
 
 def gather_kernel(
-    kept, ga_in, gb_in, meta_in, share_in, ga, gb, meta, share, part,
-    a0, a1, b0, b1, acc, words, send_sem, recv_sem, note_send, note_recv, load_sem, out_sem,
+    kept, cols, flags, x_ref, ga_in, gb_in, meta_in, ga, gb, meta, share, part,
+    a0, a1, b0, b1, own, acc, words, total, norm, send_sem, recv_sem, note_send, note_recv, load_sem, out_sem,
 ):
     row = lax.axis_index("row")
     col = lax.axis_index("col")
@@ -331,6 +304,8 @@
     for t in range(PER):
         b0[2 * TILE + t] = zero
         b1[2 * TILE + t] = zero
+    own_copy = pltpu.make_async_copy(x_ref, own, load_sem.at[2, 1])
+    own_copy.start()
     pl.semaphore_wait(barrier, 22)
     for n in range(22):
         note(n, note_slots(n)[0]).start()
@@ -367,16 +342,39 @@
             at_second = words[line, 0, 17 + spot] + half * PACKED
             left = whole(abuf, pos)
             for p in range(KEPT):
-                j = jnp.where(k >= 0, kept[i, p], -2)
+                j = jnp.where(k >= 0, kept[p, i], -2)
                 index = jnp.where(first == j, at_first, jnp.where(second == j, at_second, 2 * PACKED))
                 right = whole(bbuf, index)
                 term = jnp.dot(left, right, preferred_element_type=jnp.float32)
                 sums[p] = term if sums[p] is None else sums[p] + term
+        flag = flags[i] == 1
+        sign = jnp.where(flag, -1.0, 1.0).astype(jnp.float32)
         for p in range(KEPT):
             if n == 0:
-                acc[i * KEPT + p] = sums[p]
+                second = cols[1, i] == kept[p, i]
+                there = second | (cols[0, i] == kept[p, i])
+                scale = jnp.where(flag & there, 2.0, 0.0).astype(jnp.float32)
+                block = whole(own, i * SLOTS + jnp.where(second, 1, 0)).astype(jnp.float32)
+                acc[i * KEPT + p] = scale * block + sign * sums[p]
             else:
-                acc[i * KEPT + p] += sums[p]
+                acc[i * KEPT + p] += sign * sums[p]
+
+    def norms(i, carry):
+        sign = jnp.where(flags[i] == 1, -1.0, 1.0).astype(jnp.float32)
+        for s in range(SLOTS):
+            entry = cols[s, i]
+            weight = jnp.where(entry >= 0, sign, 0.0)
+            twice = jnp.where((flags[i] == 1) & (entry == row * ROWS + i), 2.0, 0.0)
+            block = whole(own, i * SLOTS + s).astype(jnp.float32)
+            down = lax.broadcasted_iota(jnp.int32, (BLK, BLK), 0)
+            across = lax.broadcasted_iota(jnp.int32, (BLK, BLK), 1)
+            term = weight * block * block + jnp.where(down == across, twice * block, 0.0)
+            norm[...] += jnp.sum(term.reshape(BLK // 8, 8, BLK), axis=0)
+        return carry
+
+    share_copy = pltpu.make_async_copy(
+        total, share.at[core * 64 + z * 16 + y * 4 + x], load_sem.at[2, 2]
+    )
 
     def result(i):
         piece = pl.ds(i * KEPT, GROUP * KEPT)
@@ -395,6 +393,15 @@
         if kind == "send":
             await_all(ITEMS[what]["pre"])
             outgoing(what).start()
+        elif kind == "trace":
+            own_copy.wait()
+            norm[...] = jnp.zeros_like(norm)
+            lax.fori_loop(0, ROWS, norms, 0)
+            lane = lax.broadcasted_iota(jnp.int32, (1, LANES), 1)
+            total[...] = jnp.where(lane == 0, jnp.sum(norm[...]), 0.0)
+        elif kind == "share":
+            share_copy.start()
+            share_copy.wait()
         elif kind == "rows":
             for n in range(22):
                 note(n, note_slots(n)[1]).wait_recv()
@@ -430,107 +437,108 @@
 
 
 def product_kernel(
-    meta, kept, cols, flags, share, part_ref, x_ref, ga, gb,
-    out_ref, trace_ref,
-    abuf, bbuf, acc, sem,
+    meta, kept, flags, share, part_ref, ga, gb, out_ref, trace_ref, abuf, bbuf, sem
 ):
     i = pl.program_id(0)
     x, y, z, core = place()
-
-    def loads(n):
-        c = pair_of(PAIRS - LEFT + n, x, y)
+    c = pair_of(PAIRS - 1, x, y)
+
+    def loads():
         return [
-            pltpu.make_async_copy(ga.at[c], abuf.at[n], sem.at[n, 0]),
-            pltpu.make_async_copy(gb.at[2 * c], bbuf.at[n, pl.ds(0, TILE)], sem.at[n, 1]),
-            pltpu.make_async_copy(gb.at[2 * c + 1], bbuf.at[n, pl.ds(TILE, TILE)], sem.at[n, 2]),
+            pltpu.make_async_copy(ga.at[c], abuf, sem.at[0]),
+            pltpu.make_async_copy(gb.at[2 * c], bbuf.at[pl.ds(0, TILE)], sem.at[1]),
+            pltpu.make_async_copy(gb.at[2 * c + 1], bbuf.at[pl.ds(TILE, TILE)], sem.at[2]),
         ]
 
     @pl.when(i == 0)
     def _():
-        for n in range(LEFT):
-            for copy in loads(n):
-                copy.start()
+        for copy in loads():
+            copy.start()
+        bbuf[pl.ds(2 * TILE, PER)] = jnp.zeros((PER, PART, BLK), jnp.bfloat16)
         lane = lax.broadcasted_iota(jnp.int32, (128, 1, LANES), 2)
         trace_ref[0, 0] = jnp.sum(jnp.where(lane == 0, share[...], 0.0))
-        for n in range(LEFT):
-            for copy in loads(n):
-                copy.wait()
-
-    acc[...] = part_ref[0]
-    for n in range(LEFT):
-        c = pair_of(PAIRS - LEFT + n, x, y)
-        for e in range(SLOTS):
-            k = meta[c, 0, i * SLOTS + e]
-
-            @pl.when(k >= 0)
-            def _(n=n, c=c, e=e, k=k):
-                pos = meta[c, 0, 16 + i * SLOTS + e]
-                other = k // ROWS
-                for s in range(SLOTS):
-                    spot = lax.rem(k, ROWS) * SLOTS + s
-                    j = meta[8 + other, 0, spot]
-                    p = jnp.int32(-1)
-                    for t in range(KEPT):
-                        p = jnp.where(kept[i, t] == j, t, p)
-
-                    @pl.when(p >= 0)
-                    def _(spot=spot, p=p):
-                        at = meta[8 + other, 0, 16 + spot] + (other - 2 * c) * PACKED
-                        acc[p] += jnp.dot(
-                            abuf[n, pl.ds(pos * PER, PER)].reshape(BLK, BLK),
-                            bbuf[n, pl.ds(at * PER, PER)].reshape(BLK, BLK),
-                            preferred_element_type=jnp.float32,
-                        )
-
-    flag = flags[i] == 1
-    sign = jnp.where(flag, -1.0, 1.0).astype(jnp.float32)
+        for copy in loads():
+            copy.wait()
+
+    sign = jnp.where(flags[i] == 1, -1.0, 1.0).astype(jnp.float32)
+    lines = []
+    for e in range(SLOTS):
+        k = meta[c, 0, i * SLOTS + e]
+        pos = meta[c, 0, 16 + i * SLOTS + e]
+        local = jnp.maximum(k - c * SPAN, 0)
+        half = local // ROWS
+        spot = (local - half * ROWS) * SLOTS
+        line = 8 + 2 * c + half
+        at = [meta[line, 0, 16 + spot + t] + half * PACKED for t in range(SLOTS)]
+        lines.append((k >= 0, pos, [meta[line, 0, spot + t] for t in range(SLOTS)], at))
     for p in range(KEPT):
-        j = kept[i, p]
-        second = cols[i, 1] == j
-        there = second | (cols[i, 0] == j)
-        scale = jnp.where(flag & there, 2.0, 0.0).astype(jnp.float32)
-        own = x_ref[0, second.astype(jnp.int32)].astype(jnp.float32)
-        out_ref[0, p] = (scale * own + sign * acc[p]).astype(jnp.bfloat16)
+        j = kept[p, i]
+        spots, hits = [], []
+        for live, _, names, at in lines:
+            first, second = live & (names[0] == j), live & (names[1] == j)
+            spots.append(jnp.where(first, at[0], jnp.where(second, at[1], 2 * PACKED)))
+            hits.append(first | second)
+
+        @pl.when(hits[0] | hits[1])
+        def _(p=p, spots=spots):
+            terms = [
+                jnp.dot(
+                    abuf[pl.ds(line[1] * PER, PER)].reshape(BLK, BLK),
+                    bbuf[pl.ds(spot * PER, PER)].reshape(BLK, BLK),
+                    preferred_element_type=jnp.float32,
+                )
+                for line, spot in zip(lines, spots)
+            ]
+            out_ref[0, p] = (part_ref[0, p] + sign * (terms[0] + terms[1])).astype(jnp.bfloat16)
+
+        @pl.when(jnp.logical_not(hits[0] | hits[1]))
+        def _(p=p):
+            out_ref[0, p] = part_ref[0, p].astype(jnp.bfloat16)
 
 
 def per_device(x_blocks, x_cols, out_cols, branch_flag):
     anywhere = pl.BlockSpec(memory_space=pl.ANY)
     scalars = pl.BlockSpec(memory_space=pltpu.SMEM)
+    cols, kept = x_cols.T, out_cols.T
+    blocks = x_blocks.reshape(ROWS * SLOTS * PER, PART, BLK)
     shapes = (
         jax.ShapeDtypeStruct((8, TILE, PART, BLK), jnp.bfloat16),
         jax.ShapeDtypeStruct((16, TILE, PART, BLK), jnp.bfloat16),
         jax.ShapeDtypeStruct((24, 1, LANES), jnp.int32),
-        jax.ShapeDtypeStruct((128, 1, LANES), jnp.float32),
     )
     gathered = pl.pallas_call(
         pack_kernel,
         name="pack",
         out_shape=shapes,
-        in_specs=[scalars, scalars, anywhere],
-        out_specs=[anywhere] * 4,
+        in_specs=[scalars, anywhere],
+        out_specs=[anywhere] * 3,
         scratch_shapes=[
             pltpu.VMEM((TILE, PART, BLK), jnp.bfloat16),
             pltpu.SMEM((16,), jnp.int32),
             pltpu.VMEM((1, LANES), jnp.int32),
-            pltpu.VMEM((1, LANES), jnp.float32),
-            pltpu.VMEM((8, BLK), jnp.float32),
             pltpu.SemaphoreType.DMA((PACKED,)),
-            pltpu.SemaphoreType.DMA((5,)),
+            pltpu.SemaphoreType.DMA((2 * PACKED + 2,)),
         ],
-    )(x_cols, branch_flag, x_blocks.reshape(ROWS, SLOTS, PER, PART, BLK))
+    )(cols, blocks)
     ga, gb, meta, share, part = pl.pallas_call(
         gather_kernel,
         name="gather",
-        out_shape=shapes + (jax.ShapeDtypeStruct((ROWS * KEPT, BLK, BLK), jnp.float32),),
-        in_specs=[scalars] + [anywhere] * 4,
+        out_shape=shapes + (
+            jax.ShapeDtypeStruct((128, 1, LANES), jnp.float32),
+            jax.ShapeDtypeStruct((ROWS * KEPT, BLK, BLK), jnp.float32),
+        ),
+        in_specs=[scalars] * 3 + [anywhere] * 4,
         out_specs=[anywhere] * 5,
         scratch_shapes=[
             pltpu.VMEM((TILE, PART, BLK), jnp.bfloat16),
             pltpu.VMEM((TILE, PART, BLK), jnp.bfloat16),
             pltpu.VMEM((2 * TILE + PER, PART, BLK), jnp.bfloat16),
             pltpu.VMEM((2 * TILE + PER, PART, BLK), jnp.bfloat16),
+            pltpu.VMEM((ROWS * SLOTS * PER, PART, BLK), jnp.bfloat16),
             pltpu.VMEM((ROWS * KEPT, BLK, BLK), jnp.float32),
             pltpu.SMEM((24, 1, LANES), jnp.int32),
+            pltpu.VMEM((1, LANES), jnp.float32),
+            pltpu.VMEM((8, BLK), jnp.float32),
             pltpu.SemaphoreType.DMA((len(ORDER),)),
             pltpu.SemaphoreType.DMA((len(ORDER),)),
             pltpu.SemaphoreType.DMA((22,)),
@@ -538,9 +546,9 @@
             pltpu.SemaphoreType.DMA((3, 3)),
             pltpu.SemaphoreType.DMA((ROWS // GROUP,)),
         ],
-        input_output_aliases={1: 0, 2: 1, 3: 2, 4: 3},
+        input_output_aliases={4: 0, 5: 1, 6: 2},
         compiler_params=pltpu.CompilerParams(collective_id=0, has_side_effects=True),
-    )(out_cols, *gathered)
+    )(kept, cols, branch_flag, blocks, *gathered)
     purified, trace = pl.pallas_call(
         product_kernel,
         name="product",
@@ -550,21 +558,18 @@
             jax.ShapeDtypeStruct((1, 1), jnp.float32),
         ),
         in_specs=[
-            scalars, scalars, scalars, scalars,
+            scalars, scalars, scalars,
             pl.BlockSpec((128, 1, LANES), lambda i: (0, 0, 0)),
             pl.BlockSpec((1, KEPT, BLK, BLK), lambda i: (i, 0, 0, 0)),
-            pl.BlockSpec((1, SLOTS, BLK, BLK), lambda i: (i, 0, 0, 0)),
             anywhere, anywhere,
         ],
         out_specs=[pl.BlockSpec((1, KEPT, BLK, BLK), lambda i: (i, 0, 0, 0)), scalars],
         scratch_shapes=[
-            pltpu.VMEM((LEFT, TILE, PART, BLK), jnp.bfloat16),
-            pltpu.VMEM((LEFT, 2 * TILE, PART, BLK), jnp.bfloat16),
-            pltpu.VMEM((KEPT, BLK, BLK), jnp.float32),
-            pltpu.SemaphoreType.DMA((LEFT, 3)),
+            pltpu.VMEM((TILE, PART, BLK), jnp.bfloat16),
+            pltpu.VMEM((2 * TILE + PER, PART, BLK), jnp.bfloat16),
+            pltpu.SemaphoreType.DMA((3,)),
         ],
-    )(meta, out_cols, x_cols, branch_flag, share,
-      part.reshape(ROWS, KEPT, BLK, BLK), x_blocks, ga, gb)
+    )(meta, kept, branch_flag, share, part.reshape(ROWS, KEPT, BLK, BLK), ga, gb)
     return purified, trace.reshape(1)
 
 

time: 172 us -> 168 us (0.977)
  local copies, waits for them, and re-layouts: 2.69 us -> 0 us
  Pallas kernels: 168 us -> 166 us
    unnamed x2 -> x0, local copies, waits for them, and re-layouts: 2.69 us -> none
where the time goes in v3:
time: 168 us; the launch traced here: 167 us
  Pallas kernels  166 us (99%)
    pallas_call x1, Pallas kernels, per_device(): pl.pallas_call(gather_kernel, name='gather', out_shape=shapes + (jax.Shap...  151 us
    pallas_call x1, Pallas kernels, per_device(): pl.pallas_call(product_kernel, name='product', grid=(ROWS,), out_shape=(j...  11.5 us
    pallas_call x1, Pallas kernels, per_device(): pl.pallas_call(pack_kernel, name='pack', out_shape=shapes, in_specs=[scal...  3.73 us

profile of v3, /device:TPU:2, one launch (start us, length us, event | category | flops | bytes accessed | tf_op | source)
XLA Modules:
  0.0 166.6 jit_solution(10335531570342708918)
XLA Ops:
  0.6 3.7 %pack.1 = (bf16[8,52,64,256]{3,2,1,0:T(8,128)(2,1)}, bf16[16,52,64,256]{3,2,1,0:T(8,128)(2,1)}, s32[24,1,128]{2,1,0:T(1,128)}) custom-call(s32[2,8]{1,0:T(2,128)} %bitcast.10, bf16[64,64,256]{2,1,0:T(8,128)(2,1)} %bitcast.5), custom_call_target="tpu_custom_call" | custom-call | tf_op jit(solution)/shard_map/pack/pallas_call | solution.py:509
  4.4 150.6 %gather.1 = (bf16[8,52,64,256]{3,2,1,0:T(8,128)(2,1)}, bf16[16,52,64,256]{3,2,1,0:T(8,128)(2,1)}, s32[24,1,128]{2,1,0:T(1,128)}, f32[128,1,128]{2,1,0:T(1,128)}, f32[32,256,256]{2,1,0:T(8,128)}) custom-call(s32[4,8]{1,0:T(4,128)} %bitcast.8, s32[2,8]{1,0:T(2,128)} %bitcast.11, s32[8]{0:T(128)} %flags.3, ...), custom_call_target="tpu_custom_call", output_to_operand_aliasing={{0}: (4, {}), {1}: (5, {}), {2}: (6, {})} | custom-call | tf_op jit(solution)/shard_map/gather/pallas_call | solution.py:523
  155.0 11.5 %product.1 = (bf16[8,4,256,256]{3,2,1,0:T(8,128)(2,1)}, f32[1,1]{1,0:T(1,128)}) custom-call(s32[24,1,128]{2,1,0:T(1,128)} %get-tuple-element.15.meta, s32[4,8]{1,0:T(4,128)} %bitcast.9, s32[8]{0:T(128)} %flags.3, f32[128,1,128]{2,1,0:T(1,128)} %get-tuple-element.16.share, f32[8,4,256,256]{3,2,1,0:T(8,128)} %bitcast.7, ...), custom_call_target="tpu_custom_call" | custom-call | tf_op jit(solution)/shard_map/product/pallas_call | solution.py:552

commit v4 on v3

--- a/solution.py
+++ b/solution.py
@@ -71,6 +71,15 @@
         before = before + [("M", axis + "+", 0), ("M", axis + "-", 0), ("M", axis + "+", 3)]
     items[("M", "s", 0)] = dict(link="s", size=0.02, pre=list(before))
 
+    for axis in "xyz":
+        pre = [("N", "x+", 0), ("N", "x-", 0), ("N", "x+", 3)] if axis == "y" else []
+        items[("N", axis + "+", 0)] = dict(link=axis + "+", size=0.02, pre=pre)
+        items[("N", axis + "-", 0)] = dict(link=axis + "-", size=0.02, pre=pre)
+        items[("N", axis + "+", 3)] = dict(link=axis + "+", size=0.02, pre=[("N", axis + "+", 0)])
+    items[("N", "s", 0)] = dict(
+        link="s", size=0.02, pre=[("N", "z+", 0), ("N", "z-", 0), ("N", "z+", 3)]
+    )
+
     source = {}
     for key in items:
         if key[0] == "B":
@@ -108,7 +117,7 @@
             if key[0] == "M":
                 ready = max(ready, SHARE_AT)
             at = max(ready, free[items[key]["link"]])
-            small = 0 if key[0] == "M" else 1
+            small = 0 if key[0] in "MN" else 1
             mark = (at, small, urgency(key))
             if best is None or mark < best[0]:
                 best = (mark, key, ready, at)
@@ -122,7 +131,7 @@
     events.append(((0.4, 0.0, 0), ("trace", None)))
     events.append(((SHARE_AT - LOOKAHEAD - 0.1, 0.0, 0), ("share", None)))
 
-    clock = max(landed[key] for key in items if key[0] == "A") + 0.2
+    clock = max(landed[key] for key in items if key[0] in "AN") + 0.2
     events.append(((clock, 0.0, 0), ("rows", None)))
     needs = []
     for n in range(PAIRS - LEFT):
@@ -159,6 +168,10 @@
     return lax.rem(row, RING), row // RING, col // 2, lax.rem(col, 2)
 
 
+def note_slot(col):
+    return lax.rem(col, 2) * RING + col // 2
+
+
 def turn(value, by):
     return lax.rem(value + by % RING, RING)
 
@@ -199,7 +212,7 @@
             copy = pltpu.make_async_copy(buf.at[piece], to, out_sem.at[2 * t + n])
             copy.start()
             outs.append(copy)
-    for n, slot in enumerate((col, 8 + row)):
+    for n, slot in enumerate((note_slot(col), 8 + row)):
         copy = pltpu.make_async_copy(line, meta.at[slot], out_sem.at[2 * PACKED + n])
         copy.start()
         outs.append(copy)
@@ -208,8 +221,8 @@
 
 
 def gather_kernel(
-    kept, cols, flags, x_ref, ga_in, gb_in, meta_in, ga, gb, meta, share, part,
-    a0, a1, b0, b1, own, acc, words, total, norm, send_sem, recv_sem, note_send, note_recv, load_sem, out_sem,
+    kept, cols, flags, x_ref, ga_in, gb_in, meta_in, ga, gb, meta, share, part, draft,
+    a0, a1, b0, b1, own, acc, rounded, words, total, norm, send_sem, recv_sem, load_sem, out_sem,
 ):
     row = lax.axis_index("row")
     col = lax.axis_index("col")
@@ -234,6 +247,14 @@
             slot = turn(pz, key[2]) * 2 + pcore
             return ga.at[slot, pl.ds(key[3] * CUT, CUT)]
         axis = key[1][0]
+        if key[0] == "N":
+            if axis == "x":
+                return meta.at[pl.ds(8 + py * 4 + turn(px, key[2]), 1)]
+            if axis == "y":
+                return meta.at[pl.ds(8 + turn(py, key[2]) * 4, 4)]
+            if axis == "z":
+                return meta.at[pl.ds(pcore * 4 + turn(pz, key[2]), 1)]
+            return meta.at[pl.ds(pcore * 4, 4)]
         if axis == "x":
             return share.at[pl.ds(pcore * 64 + pz * 16 + py * 4 + turn(px, key[2]), 1)]
         if axis == "y":
@@ -277,38 +298,17 @@
             device_id_type=MESH,
         )
 
-    def note_slots(n):
-        if n < 7:
-            return col, lax.rem(col + 7 - n, 8)
-        return 8 + row, 8 + lax.rem(row + 22 - n, 16)
-
-    def note_device(n):
-        if n < 7:
-            return {"row": row, "col": lax.rem(col + n + 1, 8)}
-        return {"row": lax.rem(row + n - 6, 16), "col": col}
-
-    def note(n, slot):
-        return pltpu.make_async_remote_copy(
-            src_ref=meta.at[slot],
-            dst_ref=meta.at[slot],
-            send_sem=note_send.at[n],
-            recv_sem=note_recv.at[n],
-            device_id=note_device(n),
-            device_id_type=MESH,
-        )
-
     barrier = pltpu.get_barrier_semaphore()
-    for n in range(22):
-        pl.semaphore_signal(barrier, inc=1, device_id=note_device(n), device_id_type=MESH)
+    links = ("x+", "x-", "y+", "y-", "z+", "z-", "s")
+    for link in links:
+        pl.semaphore_signal(barrier, inc=1, device_id=peer(link), device_id_type=MESH)
     zero = jnp.zeros((PART, BLK), jnp.bfloat16)
     for t in range(PER):
         b0[2 * TILE + t] = zero
         b1[2 * TILE + t] = zero
     own_copy = pltpu.make_async_copy(x_ref, own, load_sem.at[2, 1])
     own_copy.start()
-    pl.semaphore_wait(barrier, 22)
-    for n in range(22):
-        note(n, note_slots(n)[0]).start()
+    pl.semaphore_wait(barrier, len(links))
 
     def loads(n):
         c = pair_of(n, x, y)
@@ -331,8 +331,8 @@
         abuf, bbuf = (a0, b0) if n % 2 == 0 else (a1, b1)
         sums = [None] * KEPT
         for e in range(SLOTS):
-            k = words[c, 0, i * SLOTS + e]
-            pos = words[c, 0, 16 + i * SLOTS + e]
+            k = words[note_slot(c), 0, i * SLOTS + e]
+            pos = words[note_slot(c), 0, 16 + i * SLOTS + e]
             local = jnp.maximum(k - c * SPAN, 0)
             half = local // ROWS
             spot = (local - half * ROWS) * SLOTS
@@ -358,6 +358,8 @@
                 acc[i * KEPT + p] = scale * block + sign * sums[p]
             else:
                 acc[i * KEPT + p] += sign * sums[p]
+            if n == PAIRS - LEFT - 1:
+                rounded[i * KEPT + p] = acc[i * KEPT + p].astype(jnp.bfloat16)
 
     def norms(i, carry):
         sign = jnp.where(flags[i] == 1, -1.0, 1.0).astype(jnp.float32)
@@ -378,7 +380,10 @@
 
     def result(i):
         piece = pl.ds(i * KEPT, GROUP * KEPT)
-        return pltpu.make_async_copy(acc.at[piece], part.at[piece], out_sem.at[i // GROUP])
+        return [
+            pltpu.make_async_copy(acc.at[piece], part.at[piece], out_sem.at[i // GROUP, 0]),
+            pltpu.make_async_copy(rounded.at[piece], draft.at[piece], out_sem.at[i // GROUP, 1]),
+        ]
 
     seen = set()
 
@@ -403,8 +408,7 @@
             share_copy.start()
             share_copy.wait()
         elif kind == "rows":
-            for n in range(22):
-                note(n, note_slots(n)[1]).wait_recv()
+            await_all([key for key in ORDER if key[0] == "N"])
             words_copy = pltpu.make_async_copy(meta, words, load_sem.at[2, 0])
             words_copy.start()
             await_all([key for key in ORDER if key[0] == "A"])
@@ -420,14 +424,14 @@
                     copy.wait()
             lax.fori_loop(i, i + GROUP, lambda t, carry, n=n: work(n, t), None)
             if n == final:
-                result(i).start()
+                for copy in result(i):
+                    copy.start()
     await_all(ORDER)
     for i in range(0, ROWS, GROUP):
-        result(i).wait()
+        for copy in result(i):
+            copy.wait()
     for key in ORDER:
         outgoing(key).wait_send()
-    for n in range(22):
-        note(n, note_slots(n)[0]).wait_send()
 
 
 def pair_of(n, x, y):
@@ -437,63 +441,98 @@
 
 
 def product_kernel(
-    meta, kept, flags, share, part_ref, ga, gb, out_ref, trace_ref, abuf, bbuf, sem
+    meta, kept, flags, share, draft_ref, part, ga, gb, out_ref, trace_ref, abuf, bbuf, sums, sem
 ):
     i = pl.program_id(0)
     x, y, z, core = place()
     c = pair_of(PAIRS - 1, x, y)
 
-    def loads():
-        return [
-            pltpu.make_async_copy(ga.at[c], abuf, sem.at[0]),
-            pltpu.make_async_copy(gb.at[2 * c], bbuf.at[pl.ds(0, TILE)], sem.at[1]),
-            pltpu.make_async_copy(gb.at[2 * c + 1], bbuf.at[pl.ds(TILE, TILE)], sem.at[2]),
-        ]
+    def each(local, visit_left, visit_sum, visit_right):
+        lines = []
+        for e in range(SLOTS):
+            k = meta[note_slot(c), 0, local * SLOTS + e]
+            inside = jnp.maximum(k - c * SPAN, 0)
+            half = inside // ROWS
+            spot = (inside - half * ROWS) * SLOTS
+            line = 8 + 2 * c + half
+            names = [jnp.where(k >= 0, meta[line, 0, spot + t], -1) for t in range(SLOTS)]
+            at = [meta[line, 0, 16 + spot + t] for t in range(SLOTS)]
+            lines.append((2 * c + half, names, at))
+        hits = []
+        for p in range(KEPT):
+            j = kept[p, local]
+            hits.append([(names[0] == j, names[1] == j) for _, names, _ in lines])
+        for e in range(SLOTS):
+            some = hits[0][e][0] | hits[0][e][1]
+            for p in range(1, KEPT):
+                some = some | hits[p][e][0] | hits[p][e][1]
+
+            @pl.when(some)
+            def _(e=e):
+                visit_left(e, meta[note_slot(c), 0, 16 + local * SLOTS + e])
+
+        for p in range(KEPT):
+            found = [first | second for first, second in hits[p]]
+
+            @pl.when(found[0] | found[1])
+            def _(p=p, found=found):
+                visit_sum(p)
+                for e in range(SLOTS):
+
+                    @pl.when(found[e])
+                    def _(e=e):
+                        tile, _, at = lines[e]
+                        visit_right(p, e, tile, jnp.where(hits[p][e][0], at[0], at[1]))
+
+    def left(local, e, pos):
+        return pltpu.make_async_copy(
+            ga.at[c, pl.ds(pos * PER, PER)], abuf.at[local * SLOTS + e], sem.at[local]
+        )
+
+    def before(local, p):
+        n = local * KEPT + p
+        return pltpu.make_async_copy(part.at[n], sums.at[n], sem.at[local])
+
+    def right(local, p, e, tile, pos):
+        return pltpu.make_async_copy(
+            gb.at[tile, pl.ds(pos * PER, PER)],
+            bbuf.at[(local * KEPT + p) * SLOTS + e],
+            sem.at[local],
+        )
+
+    def over(local, act):
+        each(
+            local,
+            lambda e, pos: act(left(local, e, pos)),
+            lambda p: act(before(local, p)),
+            lambda p, e, tile, pos: act(right(local, p, e, tile, pos)),
+        )
 
     @pl.when(i == 0)
     def _():
-        for copy in loads():
-            copy.start()
-        bbuf[pl.ds(2 * TILE, PER)] = jnp.zeros((PER, PART, BLK), jnp.bfloat16)
+        def begin(local, carry):
+            over(local, lambda copy: copy.start())
+            return carry
+
+        lax.fori_loop(0, ROWS, begin, 0)
         lane = lax.broadcasted_iota(jnp.int32, (128, 1, LANES), 2)
         trace_ref[0, 0] = jnp.sum(jnp.where(lane == 0, share[...], 0.0))
-        for copy in loads():
-            copy.wait()
-
+
+    over(i, lambda copy: copy.wait())
+    out_ref[...] = draft_ref[...]
     sign = jnp.where(flags[i] == 1, -1.0, 1.0).astype(jnp.float32)
-    lines = []
-    for e in range(SLOTS):
-        k = meta[c, 0, i * SLOTS + e]
-        pos = meta[c, 0, 16 + i * SLOTS + e]
-        local = jnp.maximum(k - c * SPAN, 0)
-        half = local // ROWS
-        spot = (local - half * ROWS) * SLOTS
-        line = 8 + 2 * c + half
-        at = [meta[line, 0, 16 + spot + t] + half * PACKED for t in range(SLOTS)]
-        lines.append((k >= 0, pos, [meta[line, 0, spot + t] for t in range(SLOTS)], at))
-    for p in range(KEPT):
-        j = kept[p, i]
-        spots, hits = [], []
-        for live, _, names, at in lines:
-            first, second = live & (names[0] == j), live & (names[1] == j)
-            spots.append(jnp.where(first, at[0], jnp.where(second, at[1], 2 * PACKED)))
-            hits.append(first | second)
-
-        @pl.when(hits[0] | hits[1])
-        def _(p=p, spots=spots):
-            terms = [
-                jnp.dot(
-                    abuf[pl.ds(line[1] * PER, PER)].reshape(BLK, BLK),
-                    bbuf[pl.ds(spot * PER, PER)].reshape(BLK, BLK),
-                    preferred_element_type=jnp.float32,
-                )
-                for line, spot in zip(lines, spots)
-            ]
-            out_ref[0, p] = (part_ref[0, p] + sign * (terms[0] + terms[1])).astype(jnp.bfloat16)
-
-        @pl.when(jnp.logical_not(hits[0] | hits[1]))
-        def _(p=p):
-            out_ref[0, p] = part_ref[0, p].astype(jnp.bfloat16)
+
+    def multiply(p, e, tile, pos):
+        n = i * KEPT + p
+        total = sums[n] + sign * jnp.dot(
+            abuf[i * SLOTS + e].reshape(BLK, BLK),
+            bbuf[n * SLOTS + e].reshape(BLK, BLK),
+            preferred_element_type=jnp.float32,
+        )
+        sums[n] = total
+        out_ref[0, p] = total.astype(jnp.bfloat16)
+
+    each(i, lambda e, pos: None, lambda p: None, multiply)
 
 
 def per_device(x_blocks, x_cols, out_cols, branch_flag):
@@ -520,15 +559,16 @@
             pltpu.SemaphoreType.DMA((2 * PACKED + 2,)),
         ],
     )(cols, blocks)
-    ga, gb, meta, share, part = pl.pallas_call(
+    ga, gb, meta, share, part, draft = pl.pallas_call(
         gather_kernel,
         name="gather",
         out_shape=shapes + (
             jax.ShapeDtypeStruct((128, 1, LANES), jnp.float32),
             jax.ShapeDtypeStruct((ROWS * KEPT, BLK, BLK), jnp.float32),
+            jax.ShapeDtypeStruct((ROWS * KEPT, BLK, BLK), jnp.bfloat16),
         ),
         in_specs=[scalars] * 3 + [anywhere] * 4,
-        out_specs=[anywhere] * 5,
+        out_specs=[anywhere] * 6,
         scratch_shapes=[
             pltpu.VMEM((TILE, PART, BLK), jnp.bfloat16),
             pltpu.VMEM((TILE, PART, BLK), jnp.bfloat16),
@@ -536,15 +576,14 @@
             pltpu.VMEM((2 * TILE + PER, PART, BLK), jnp.bfloat16),
             pltpu.VMEM((ROWS * SLOTS * PER, PART, BLK), jnp.bfloat16),
             pltpu.VMEM((ROWS * KEPT, BLK, BLK), jnp.float32),
+            pltpu.VMEM((ROWS * KEPT, BLK, BLK), jnp.bfloat16),
             pltpu.SMEM((24, 1, LANES), jnp.int32),
             pltpu.VMEM((1, LANES), jnp.float32),
             pltpu.VMEM((8, BLK), jnp.float32),
             pltpu.SemaphoreType.DMA((len(ORDER),)),
             pltpu.SemaphoreType.DMA((len(ORDER),)),
-            pltpu.SemaphoreType.DMA((22,)),
-            pltpu.SemaphoreType.DMA((22,)),
             pltpu.SemaphoreType.DMA((3, 3)),
-            pltpu.SemaphoreType.DMA((ROWS // GROUP,)),
+            pltpu.SemaphoreType.DMA((ROWS // GROUP, 2)),
         ],
         input_output_aliases={4: 0, 5: 1, 6: 2},
         compiler_params=pltpu.CompilerParams(collective_id=0, has_side_effects=True),
@@ -561,15 +600,16 @@
             scalars, scalars, scalars,
             pl.BlockSpec((128, 1, LANES), lambda i: (0, 0, 0)),
             pl.BlockSpec((1, KEPT, BLK, BLK), lambda i: (i, 0, 0, 0)),
-            anywhere, anywhere,
+            anywhere, anywhere, anywhere,
         ],
         out_specs=[pl.BlockSpec((1, KEPT, BLK, BLK), lambda i: (i, 0, 0, 0)), scalars],
         scratch_shapes=[
-            pltpu.VMEM((TILE, PART, BLK), jnp.bfloat16),
-            pltpu.VMEM((2 * TILE + PER, PART, BLK), jnp.bfloat16),
-            pltpu.SemaphoreType.DMA((3,)),
+            pltpu.VMEM((ROWS * SLOTS, PER, PART, BLK), jnp.bfloat16),
+            pltpu.VMEM((ROWS * KEPT * SLOTS, PER, PART, BLK), jnp.bfloat16),
+            pltpu.VMEM((ROWS * KEPT, BLK, BLK), jnp.float32),
+            pltpu.SemaphoreType.DMA((ROWS,)),
         ],
-    )(meta, kept, branch_flag, share, part.reshape(ROWS, KEPT, BLK, BLK), ga, gb)
+    )(meta, kept, branch_flag, share, draft.reshape(ROWS, KEPT, BLK, BLK), part, ga, gb)
     return purified, trace.reshape(1)
 
 

time: 168 us -> 166 us (0.988)
  Pallas kernels: 166 us -> 164 us
where the time goes in v4:
time: 166 us; the launch traced here: 165 us
  Pallas kernels  164 us (99%)
    pallas_call x1, Pallas kernels, per_device(): pl.pallas_call(gather_kernel, name='gather', out_shape=shapes + (jax.Shap...  149 us
    pallas_call x1, Pallas kernels, per_device(): pl.pallas_call(product_kernel, name='product', grid=(ROWS,), out_shape=(j...  10.3 us
    pallas_call x1, Pallas kernels, per_device(): pl.pallas_call(pack_kernel, name='pack', out_shape=shapes, in_specs=[scal...  4.3 us

profile of v4, /device:TPU:2, one launch (start us, length us, event | category | flops | bytes accessed | tf_op | source)
XLA Modules:
  0.0 164.7 jit_solution(4948512040969995190)
XLA Ops:
  0.6 4.3 %pack.1 = (bf16[8,52,64,256]{3,2,1,0:T(8,128)(2,1)}, bf16[16,52,64,256]{3,2,1,0:T(8,128)(2,1)}, s32[24,1,128]{2,1,0:T(1,128)}) custom-call(s32[2,8]{1,0:T(2,128)} %bitcast.10, bf16[64,64,256]{2,1,0:T(8,128)(2,1)} %bitcast.5), custom_call_target="tpu_custom_call" | custom-call | tf_op jit(solution)/shard_map/pack/pallas_call | solution.py:548
  4.9 149.4 %gather.1 = (bf16[8,52,64,256]{3,2,1,0:T(8,128)(2,1)}, bf16[16,52,64,256]{3,2,1,0:T(8,128)(2,1)}, s32[24,1,128]{2,1,0:T(1,128)}, f32[128,1,128]{2,1,0:T(1,128)},...) custom-call(s32[4,8]{1,0:T(4,128)} %bitcast.8, ...), custom_call_target="tpu_custom_call", output_to_operand_aliasing={{0}: (4, {}), {1}: (5, {}), {2}: (6, {})} | custom-call | tf_op jit(solution)/shard_map/gather/pallas_call | solution.py:562
  154.4 10.3 %product.1 = (bf16[8,4,256,256]{3,2,1,0:T(8,128)(2,1)}, f32[1,1]{1,0:T(1,128)}) custom-call(s32[24,1,128]{2,1,0:T(1,128)} %get-tuple-element.16.meta, s32[4,8]{1,0:T(4,128)} %bitcast.9, s32[8]{0:T(128)} %flags.3, f32[128,1,128]{2,1,0:T(1,128)} %get-tuple-element.17.share, bf16[8,4,256,256]{3,2,1,0:T(8,128)(2,1)} %bitcast.7, ...), custom_call_target="tpu_custom_call" | custom-call | tf_op jit(solution)/shard_map/product/pallas_call | solution.py:591

commit v5 on v4

--- a/solution.py
+++ b/solution.py
@@ -176,53 +176,9 @@
     return lax.rem(value + by % RING, RING)
 
 
-def pack_kernel(cols, x_ref, ga, gb, meta, buf, source, line, in_sem, out_sem):
-    row = lax.axis_index("row")
-    col = lax.axis_index("col")
-    for t in range(PACKED):
-        source[t] = 0
-    lane = lax.broadcasted_iota(jnp.int32, (1, LANES), 1)
-    count = jnp.int32(0)
-    info = jnp.zeros((1, LANES), jnp.int32)
-    for s in range(ROWS * SLOTS):
-        entry = cols[s % SLOTS, s // SLOTS]
-        live = entry >= 0
-
-        @pl.when(live)
-        def _(s=s, count=count):
-            source[count] = s
-
-        info = jnp.where(lane == s, entry, info)
-        info = jnp.where(lane == 16 + s, jnp.where(live, count, 0), info)
-        count = count + live.astype(jnp.int32)
-
-    def fetch(t):
-        return pltpu.make_async_copy(
-            x_ref.at[pl.ds(source[t] * PER, PER)], buf.at[pl.ds(t * PER, PER)], in_sem.at[t]
-        )
-
-    for t in range(PACKED):
-        fetch(t).start()
-    line[...] = info
-    outs = []
-    for t in range(PACKED):
-        fetch(t).wait()
-        piece = pl.ds(t * PER, PER)
-        for n, to in enumerate((gb.at[row, piece], ga.at[col, piece])):
-            copy = pltpu.make_async_copy(buf.at[piece], to, out_sem.at[2 * t + n])
-            copy.start()
-            outs.append(copy)
-    for n, slot in enumerate((note_slot(col), 8 + row)):
-        copy = pltpu.make_async_copy(line, meta.at[slot], out_sem.at[2 * PACKED + n])
-        copy.start()
-        outs.append(copy)
-    for copy in outs:
-        copy.wait()
-
-
 def gather_kernel(
-    kept, cols, flags, x_ref, ga_in, gb_in, meta_in, ga, gb, meta, share, part, draft,
-    a0, a1, b0, b1, own, acc, rounded, words, total, norm, send_sem, recv_sem, load_sem, out_sem,
+    kept, cols, flags, x_ref, ga, gb, meta, share, part, draft,
+    a0, a1, b0, b1, own, packed, line, acc, rounded, words, total, norm, send_sem, recv_sem, load_sem, out_sem,
 ):
     row = lax.axis_index("row")
     col = lax.axis_index("col")
@@ -302,13 +258,42 @@
     links = ("x+", "x-", "y+", "y-", "z+", "z-", "s")
     for link in links:
         pl.semaphore_signal(barrier, inc=1, device_id=peer(link), device_id_type=MESH)
+    own_copy = pltpu.make_async_copy(x_ref, own, load_sem.at[2, 1])
+    own_copy.start()
+
+    lane = lax.broadcasted_iota(jnp.int32, (1, LANES), 1)
+    count = jnp.int32(0)
+    info = jnp.zeros((1, LANES), jnp.int32)
+    source = [jnp.int32(0)] * PACKED
+    for s in range(ROWS * SLOTS):
+        entry = cols[s % SLOTS, s // SLOTS]
+        live = entry >= 0
+        info = jnp.where(lane == s, entry, info)
+        info = jnp.where(lane == 16 + s, jnp.where(live & (count < PACKED), count, 0), info)
+        for t in range(max(0, s - ROWS * SLOTS + 1), min(s + 1, PACKED)):
+            source[t] = jnp.where(live & (count == t), s, source[t])
+        count = count + jnp.where(live, 1, 0)
+    line[...] = info
+    own_copy.wait()
+    for t in range(PACKED):
+        for h in range(PER):
+            packed[t * PER + h] = own[source[t] * PER + h]
     zero = jnp.zeros((PART, BLK), jnp.bfloat16)
     for t in range(PER):
         b0[2 * TILE + t] = zero
         b1[2 * TILE + t] = zero
-    own_copy = pltpu.make_async_copy(x_ref, own, load_sem.at[2, 1])
-    own_copy.start()
+    norm[...] = jnp.zeros_like(norm)
+    first = [
+        pltpu.make_async_copy(line, meta.at[note_slot(col)], load_sem.at[0, 0]),
+        pltpu.make_async_copy(line, meta.at[8 + row], load_sem.at[0, 1]),
+        pltpu.make_async_copy(packed, gb.at[row], load_sem.at[1, 0]),
+        pltpu.make_async_copy(packed, ga.at[col], load_sem.at[1, 1]),
+    ]
+    for copy in first:
+        copy.start()
     pl.semaphore_wait(barrier, len(links))
+    for copy in first:
+        copy.wait()
 
     def loads(n):
         c = pair_of(n, x, y)
@@ -399,8 +384,6 @@
             await_all(ITEMS[what]["pre"])
             outgoing(what).start()
         elif kind == "trace":
-            own_copy.wait()
-            norm[...] = jnp.zeros_like(norm)
             lax.fori_loop(0, ROWS, norms, 0)
             lane = lax.broadcasted_iota(jnp.int32, (1, LANES), 1)
             total[...] = jnp.where(lane == 0, jnp.sum(norm[...]), 0.0)
@@ -441,98 +424,126 @@
 
 
 def product_kernel(
-    meta, kept, flags, share, draft_ref, part, ga, gb, out_ref, trace_ref, abuf, bbuf, sums, sem
+    meta, kept, flags, share, draft, part, ga, gb, out, trace_ref,
+    abuf, bbuf, sums, buf, touched, place_a, place_c, counts, in_sem, get_sem, out_sem,
 ):
-    i = pl.program_id(0)
     x, y, z, core = place()
     c = pair_of(PAIRS - 1, x, y)
 
-    def each(local, visit_left, visit_sum, visit_right):
-        lines = []
+    def through(i):
+        piece = pl.ds(i * KEPT, KEPT)
+        return pltpu.make_async_copy(draft.at[piece], buf.at[piece], in_sem.at[i])
+
+    def write(n):
+        return pltpu.make_async_copy(buf.at[n], out.at[n], out_sem)
+
+    def block(tile, pos, to, i):
+        return pltpu.make_async_copy(tile.at[pl.ds(pos * PER, PER)], to, get_sem.at[i, 0])
+
+    def before(n, i):
+        return pltpu.make_async_copy(part.at[n], sums.at[n], get_sem.at[i, 1])
+
+    for i in range(ROWS):
+        through(i).start()
+
+    def begin(i, found):
+        start = found
+        lefts, blocks = jnp.int32(0), jnp.int32(0)
+        for p in range(KEPT):
+            touched[i * KEPT + p] = 0
         for e in range(SLOTS):
-            k = meta[note_slot(c), 0, local * SLOTS + e]
+            k = meta[note_slot(c), 0, i * SLOTS + e]
+            pos = meta[note_slot(c), 0, 16 + i * SLOTS + e]
             inside = jnp.maximum(k - c * SPAN, 0)
             half = inside // ROWS
             spot = (inside - half * ROWS) * SLOTS
-            line = 8 + 2 * c + half
-            names = [jnp.where(k >= 0, meta[line, 0, spot + t], -1) for t in range(SLOTS)]
-            at = [meta[line, 0, 16 + spot + t] for t in range(SLOTS)]
-            lines.append((2 * c + half, names, at))
-        hits = []
+            at = 8 + 2 * c + half
+            base = found
+            for t in range(SLOTS):
+                j = jnp.where(k >= 0, meta[at, 0, spot + t], -1)
+                p = jnp.int32(-1)
+                for o in range(KEPT):
+                    p = jnp.where(kept[o, i] == j, o, p)
+                hit = p >= 0
+
+                @pl.when(hit)
+                def _(found=found, p=p, t=t, at=at, half=half, spot=spot, e=e):
+                    n = i * KEPT + p
+                    place_a[found] = i * SLOTS + e
+                    place_c[found] = n
+                    block(gb.at[2 * c + half], meta[at, 0, 16 + spot + t], bbuf.at[found], i).start()
+
+                    @pl.when(touched[n] == 0)
+                    def _():
+                        before(n, i).start()
+                        touched[n] = 1
+
+                found = found + hit.astype(jnp.int32)
+
+            @pl.when(found > base)
+            def _(pos=pos, e=e):
+                block(ga.at[c], pos, abuf.at[i * SLOTS + e], i).start()
+
+            lefts = lefts + (found > base).astype(jnp.int32)
         for p in range(KEPT):
-            j = kept[p, local]
-            hits.append([(names[0] == j, names[1] == j) for _, names, _ in lines])
-        for e in range(SLOTS):
-            some = hits[0][e][0] | hits[0][e][1]
-            for p in range(1, KEPT):
-                some = some | hits[p][e][0] | hits[p][e][1]
-
-            @pl.when(some)
-            def _(e=e):
-                visit_left(e, meta[note_slot(c), 0, 16 + local * SLOTS + e])
-
+            blocks = blocks + touched[i * KEPT + p]
+        counts[i, 0] = start
+        counts[i, 1] = found
+        counts[i, 2] = found - start + lefts
+        counts[i, 3] = blocks
+        return found
+
+    lax.fori_loop(0, ROWS, begin, jnp.int32(0))
+
+    def pass_on(i, carry):
+        through(i).wait()
         for p in range(KEPT):
-            found = [first | second for first, second in hits[p]]
-
-            @pl.when(found[0] | found[1])
-            def _(p=p, found=found):
-                visit_sum(p)
-                for e in range(SLOTS):
-
-                    @pl.when(found[e])
-                    def _(e=e):
-                        tile, _, at = lines[e]
-                        visit_right(p, e, tile, jnp.where(hits[p][e][0], at[0], at[1]))
-
-    def left(local, e, pos):
-        return pltpu.make_async_copy(
-            ga.at[c, pl.ds(pos * PER, PER)], abuf.at[local * SLOTS + e], sem.at[local]
-        )
-
-    def before(local, p):
-        n = local * KEPT + p
-        return pltpu.make_async_copy(part.at[n], sums.at[n], sem.at[local])
-
-    def right(local, p, e, tile, pos):
-        return pltpu.make_async_copy(
-            gb.at[tile, pl.ds(pos * PER, PER)],
-            bbuf.at[(local * KEPT + p) * SLOTS + e],
-            sem.at[local],
-        )
-
-    def over(local, act):
-        each(
-            local,
-            lambda e, pos: act(left(local, e, pos)),
-            lambda p: act(before(local, p)),
-            lambda p, e, tile, pos: act(right(local, p, e, tile, pos)),
-        )
-
-    @pl.when(i == 0)
-    def _():
-        def begin(local, carry):
-            over(local, lambda copy: copy.start())
-            return carry
-
-        lax.fori_loop(0, ROWS, begin, 0)
-        lane = lax.broadcasted_iota(jnp.int32, (128, 1, LANES), 2)
-        trace_ref[0, 0] = jnp.sum(jnp.where(lane == 0, share[...], 0.0))
-
-    over(i, lambda copy: copy.wait())
-    out_ref[...] = draft_ref[...]
-    sign = jnp.where(flags[i] == 1, -1.0, 1.0).astype(jnp.float32)
-
-    def multiply(p, e, tile, pos):
-        n = i * KEPT + p
-        total = sums[n] + sign * jnp.dot(
-            abuf[i * SLOTS + e].reshape(BLK, BLK),
-            bbuf[n * SLOTS + e].reshape(BLK, BLK),
-            preferred_element_type=jnp.float32,
-        )
-        sums[n] = total
-        out_ref[0, p] = total.astype(jnp.bfloat16)
-
-    each(i, lambda e, pos: None, lambda p: None, multiply)
+
+            @pl.when(touched[i * KEPT + p] == 0)
+            def _(p=p):
+                write(i * KEPT + p).start()
+
+        return carry
+
+    lax.fori_loop(0, ROWS, pass_on, 0)
+    lane = lax.broadcasted_iota(jnp.int32, (128, 1, LANES), 2)
+    trace_ref[0, 0] = jnp.sum(jnp.where(lane == 0, share[...], 0.0))
+
+    def finish(i, carry):
+        def drain_blocks(_, inner):
+            block(ga.at[c], 0, abuf.at[0], i).wait()
+            return inner
+
+        def drain_sums(_, inner):
+            before(0, i).wait()
+            return inner
+
+        lax.fori_loop(0, counts[i, 2], drain_blocks, 0)
+        lax.fori_loop(0, counts[i, 3], drain_sums, 0)
+        sign = jnp.where(flags[i] == 1, -1.0, 1.0).astype(jnp.float32)
+
+        def multiply(t, inner):
+            n = place_c[t]
+            sums[n] += sign * jnp.dot(
+                abuf[place_a[t]].reshape(BLK, BLK),
+                bbuf[t].reshape(BLK, BLK),
+                preferred_element_type=jnp.float32,
+            )
+            return inner
+
+        lax.fori_loop(counts[i, 0], counts[i, 1], multiply, 0)
+        for p in range(KEPT):
+
+            @pl.when(touched[i * KEPT + p] == 1)
+            def _(p=p):
+                n = i * KEPT + p
+                buf[n] = sums[n].astype(jnp.bfloat16)
+                write(n).start()
+
+        return carry
+
+    lax.fori_loop(0, ROWS, finish, 0)
+    pltpu.make_async_copy(buf, out, out_sem).wait()
 
 
 def per_device(x_blocks, x_cols, out_cols, branch_flag):
@@ -545,20 +556,6 @@
         jax.ShapeDtypeStruct((16, TILE, PART, BLK), jnp.bfloat16),
         jax.ShapeDtypeStruct((24, 1, LANES), jnp.int32),
     )
-    gathered = pl.pallas_call(
-        pack_kernel,
-        name="pack",
-        out_shape=shapes,
-        in_specs=[scalars, anywhere],
-        out_specs=[anywhere] * 3,
-        scratch_shapes=[
-            pltpu.VMEM((TILE, PART, BLK), jnp.bfloat16),
-            pltpu.SMEM((16,), jnp.int32),
-            pltpu.VMEM((1, LANES), jnp.int32),
-            pltpu.SemaphoreType.DMA((PACKED,)),
-            pltpu.SemaphoreType.DMA((2 * PACKED + 2,)),
-        ],
-    )(cols, blocks)
     ga, gb, meta, share, part, draft = pl.pallas_call(
         gather_kernel,
         name="gather",
@@ -567,7 +564,7 @@
             jax.ShapeDtypeStruct((ROWS * KEPT, BLK, BLK), jnp.float32),
             jax.ShapeDtypeStruct((ROWS * KEPT, BLK, BLK), jnp.bfloat16),
         ),
-        in_specs=[scalars] * 3 + [anywhere] * 4,
+        in_specs=[scalars] * 3 + [anywhere],
         out_specs=[anywhere] * 6,
         scratch_shapes=[
             pltpu.VMEM((TILE, PART, BLK), jnp.bfloat16),
@@ -575,6 +572,8 @@
             pltpu.VMEM((2 * TILE + PER, PART, BLK), jnp.bfloat16),
             pltpu.VMEM((2 * TILE + PER, PART, BLK), jnp.bfloat16),
             pltpu.VMEM((ROWS * SLOTS * PER, PART, BLK), jnp.bfloat16),
+            pltpu.VMEM((TILE, PART, BLK), jnp.bfloat16),
+            pltpu.VMEM((1, LANES), jnp.int32),
             pltpu.VMEM((ROWS * KEPT, BLK, BLK), jnp.float32),
             pltpu.VMEM((ROWS * KEPT, BLK, BLK), jnp.bfloat16),
             pltpu.SMEM((24, 1, LANES), jnp.int32),
@@ -585,32 +584,32 @@
             pltpu.SemaphoreType.DMA((3, 3)),
             pltpu.SemaphoreType.DMA((ROWS // GROUP, 2)),
         ],
-        input_output_aliases={4: 0, 5: 1, 6: 2},
         compiler_params=pltpu.CompilerParams(collective_id=0, has_side_effects=True),
-    )(kept, cols, branch_flag, blocks, *gathered)
+    )(kept, cols, branch_flag, blocks)
     purified, trace = pl.pallas_call(
         product_kernel,
         name="product",
-        grid=(ROWS,),
         out_shape=(
-            jax.ShapeDtypeStruct((ROWS, KEPT, BLK, BLK), jnp.bfloat16),
+            jax.ShapeDtypeStruct((ROWS * KEPT, BLK, BLK), jnp.bfloat16),
             jax.ShapeDtypeStruct((1, 1), jnp.float32),
         ),
-        in_specs=[
-            scalars, scalars, scalars,
-            pl.BlockSpec((128, 1, LANES), lambda i: (0, 0, 0)),
-            pl.BlockSpec((1, KEPT, BLK, BLK), lambda i: (i, 0, 0, 0)),
-            anywhere, anywhere, anywhere,
-        ],
-        out_specs=[pl.BlockSpec((1, KEPT, BLK, BLK), lambda i: (i, 0, 0, 0)), scalars],
+        in_specs=[scalars] * 3 + [pl.BlockSpec(memory_space=pltpu.VMEM)] + [anywhere] * 4,
+        out_specs=[anywhere, scalars],
         scratch_shapes=[
             pltpu.VMEM((ROWS * SLOTS, PER, PART, BLK), jnp.bfloat16),
-            pltpu.VMEM((ROWS * KEPT * SLOTS, PER, PART, BLK), jnp.bfloat16),
+            pltpu.VMEM((ROWS * SLOTS * SLOTS, PER, PART, BLK), jnp.bfloat16),
             pltpu.VMEM((ROWS * KEPT, BLK, BLK), jnp.float32),
+            pltpu.VMEM((ROWS * KEPT, BLK, BLK), jnp.bfloat16),
+            pltpu.SMEM((ROWS * KEPT,), jnp.int32),
+            pltpu.SMEM((ROWS * SLOTS * SLOTS,), jnp.int32),
+            pltpu.SMEM((ROWS * SLOTS * SLOTS,), jnp.int32),
+            pltpu.SMEM((ROWS, 4), jnp.int32),
             pltpu.SemaphoreType.DMA((ROWS,)),
+            pltpu.SemaphoreType.DMA((ROWS, 2)),
+            pltpu.SemaphoreType.DMA,
         ],
-    )(meta, kept, branch_flag, share, draft.reshape(ROWS, KEPT, BLK, BLK), part, ga, gb)
-    return purified, trace.reshape(1)
+    )(meta, kept, branch_flag, share, draft, part, ga, gb)
+    return purified.reshape(ROWS, KEPT, BLK, BLK), trace.reshape(1)
 
 
 def solution(mesh):

time: 166 us -> 161 us (0.970)
  Pallas kernels: 164 us -> 160 us
    pallas_call x2 -> x1, Pallas kernels: 14.6 us -> 9.9 us  [per_device(): pl.pallas_call(product_kernel, name='product', out_shape=(jax.ShapeDtypeS...]
where the time goes in v5:
time: 161 us; the launch traced here: 160 us
  Pallas kernels  160 us (99%)
    pallas_call x1, Pallas kernels, per_device(): pl.pallas_call(gather_kernel, name='gather', out_shape=shapes + (jax.Shap...  150 us
    pallas_call x1, Pallas kernels, per_device(): pl.pallas_call(product_kernel, name='product', out_shape=(jax.ShapeDtypeS...  9.9 us

profile of v5, /device:TPU:2, one launch (start us, length us, event | category | flops | bytes accessed | tf_op | source)
XLA Modules:
  0.0 160.5 jit_solution(16988632405793356313)
XLA Ops:
  0.6 149.9 %gather.1 = (bf16[8,52,64,256]{3,2,1,0:T(8,128)(2,1)}, bf16[16,52,64,256]{3,2,1,0:T(8,128)(2,1)}, s32[24,1,128]{2,1,0:T(1,128)}, f32[128,1,128]{2,1,0:T(1,128)},...) custom-call(s32[4,8]{1,0:T(4,128)} %bitcast.6, s32[2,8]{1,0:T(2,128)} %bitcast.8, s32[8]{0:T(128)} %flags.3, ...), custom_call_target="tpu_custom_call" | custom-call | tf_op jit(solution)/shard_map/gather/pallas_call | solution.py:559
  150.6 9.9 %product.1 = (bf16[32,256,256]{2,1,0:T(8,128)(2,1)}, f32[1,1]{1,0:T(1,128)}) custom-call(s32[24,1,128]{2,1,0:T(1,128)} %get-tuple-element.10.meta, s32[4,8]{1,0:T(4,128)} %bitcast.7, s32[8]{0:T(128)} %flags.3, f32[128,1,128]{2,1,0:T(1,128)} %get-tuple-element.11.share, bf16[32,256,256]{2,1,0:T(8,128)(2,1)} %get-tuple-element.12.draft, ...), custom_call_target="tpu_custom_call" | custom-call | tf_op jit(solution)/shard_map/product/pallas_call | solution.py:589

commit v6 on v5

--- a/solution.py
+++ b/solution.py
@@ -155,7 +155,7 @@
 LEFT = 1
 LINE_ORDER = (0, 1, 3, 2)
 DEADLINES = (2.0, 3.0, 6.0, 7.0, 10.0, 11.0, 14.0, 15.0)
-SLACK = 0.5
+SLACK = 0.25
 CHUNK = 0.13
 GROUP = 4
 EVENTS, ORDER, ITEMS, NEEDS, PLAN_SLOTS, PLAN_WORK = build_plan()
@@ -283,17 +283,22 @@
         b0[2 * TILE + t] = zero
         b1[2 * TILE + t] = zero
     norm[...] = jnp.zeros_like(norm)
-    first = [
-        pltpu.make_async_copy(line, meta.at[note_slot(col)], load_sem.at[0, 0]),
-        pltpu.make_async_copy(line, meta.at[8 + row], load_sem.at[0, 1]),
-        pltpu.make_async_copy(packed, gb.at[row], load_sem.at[1, 0]),
-        pltpu.make_async_copy(packed, ga.at[col], load_sem.at[1, 1]),
-    ]
-    for copy in first:
+    placed = {
+        "B": [pltpu.make_async_copy(packed, gb.at[row], load_sem.at[1, 0])],
+        "N": [
+            pltpu.make_async_copy(line, meta.at[note_slot(col)], load_sem.at[0, 0]),
+            pltpu.make_async_copy(line, meta.at[8 + row], load_sem.at[0, 1]),
+        ],
+        "A": [pltpu.make_async_copy(packed, ga.at[col], load_sem.at[1, 1])],
+    }
+    for kind in "BN":
+        for copy in placed[kind]:
+            copy.start()
+    pl.semaphore_wait(barrier, len(links))
+    for copy in placed.pop("B"):
+        copy.wait()
+    for copy in placed["A"]:
         copy.start()
-    pl.semaphore_wait(barrier, len(links))
-    for copy in first:
-        copy.wait()
 
     def loads(n):
         c = pair_of(n, x, y)
@@ -381,6 +386,8 @@
     final = PAIRS - LEFT - 1
     for kind, what in EVENTS:
         if kind == "send":
+            for copy in placed.pop(what[0], []):
+                copy.wait()
             await_all(ITEMS[what]["pre"])
             outgoing(what).start()
         elif kind == "trace":
@@ -509,40 +516,61 @@
     lane = lax.broadcasted_iota(jnp.int32, (128, 1, LANES), 2)
     trace_ref[0, 0] = jnp.sum(jnp.where(lane == 0, share[...], 0.0))
 
-    def finish(i, carry):
-        def drain_blocks(_, inner):
-            block(ga.at[c], 0, abuf.at[0], i).wait()
+    def term(t):
+        n = place_c[t]
+        sign = jnp.where(flags[n // KEPT] == 1, -1.0, 1.0).astype(jnp.float32)
+        return n, sign * jnp.dot(
+            abuf[place_a[t]].reshape(BLK, BLK),
+            bbuf[t].reshape(BLK, BLK),
+            preferred_element_type=jnp.float32,
+        )
+
+    def finish(g, carry):
+        def drain_blocks(i):
+            def drain(_, inner):
+                block(ga.at[c], 0, abuf.at[0], i).wait()
+                return inner
+
+            lax.fori_loop(0, counts[i, 2], drain, 0)
+
+        def drain_sums(i):
+            def drain(_, inner):
+                before(0, i).wait()
+                return inner
+
+            lax.fori_loop(0, counts[i, 3], drain, 0)
+
+        for r in range(2):
+            drain_blocks(2 * g + r)
+            drain_sums(2 * g + r)
+        start, stop = counts[2 * g, 0], counts[2 * g + 1, 1]
+        half = (stop - start) // 2
+
+        def two(h, inner):
+            (n, first), (m, second) = term(start + 2 * h), term(start + 2 * h + 1)
+            sums[n] += first
+            sums[m] += second
             return inner
 
-        def drain_sums(_, inner):
-            before(0, i).wait()
-            return inner
-
-        lax.fori_loop(0, counts[i, 2], drain_blocks, 0)
-        lax.fori_loop(0, counts[i, 3], drain_sums, 0)
-        sign = jnp.where(flags[i] == 1, -1.0, 1.0).astype(jnp.float32)
-
-        def multiply(t, inner):
-            n = place_c[t]
-            sums[n] += sign * jnp.dot(
-                abuf[place_a[t]].reshape(BLK, BLK),
-                bbuf[t].reshape(BLK, BLK),
-                preferred_element_type=jnp.float32,
-            )
-            return inner
-
-        lax.fori_loop(counts[i, 0], counts[i, 1], multiply, 0)
-        for p in range(KEPT):
-
-            @pl.when(touched[i * KEPT + p] == 1)
-            def _(p=p):
-                n = i * KEPT + p
+        lax.fori_loop(0, half, two, 0)
+
+        @pl.when(start + 2 * half < stop)
+        def _():
+            n, first = term(stop - 1)
+            sums[n] += first
+
+        def put(n, inner):
+
+            @pl.when(touched[n] == 1)
+            def _():
                 buf[n] = sums[n].astype(jnp.bfloat16)
                 write(n).start()
 
-        return carry
-
-    lax.fori_loop(0, ROWS, finish, 0)
+            return inner
+
+        return lax.fori_loop(2 * g * KEPT, 2 * (g + 1) * KEPT, put, carry)
+
+    lax.fori_loop(0, ROWS // 2, finish, 0)
     pltpu.make_async_copy(buf, out, out_sem).wait()
 
 

time: 161 us -> 162 us (level)
  no operation moved by 1% of the time
where the time goes in v6:
time: 162 us; the launch traced here: 160 us
  Pallas kernels  160 us (99%)
    pallas_call x1, Pallas kernels, per_device(): pl.pallas_call(gather_kernel, name='gather', out_shape=shapes + (jax.Shap...  151 us
    pallas_call x1, Pallas kernels, per_device(): pl.pallas_call(product_kernel, name='product', out_shape=(jax.ShapeDtypeS...  8.66 us

profile of v6, /device:TPU:2, one launch (start us, length us, event | category | flops | bytes accessed | tf_op | source)
XLA Modules:
  0.0 160.5 jit_solution(8385987262471523064)
XLA Ops:
  0.6 151.2 %gather.1 = (bf16[8,52,64,256]{3,2,1,0:T(8,128)(2,1)}, bf16[16,52,64,256]{3,2,1,0:T(8,128)(2,1)}, s32[24,1,128]{2,1,0:T(1,128)}, f32[128,1,128]{2,1,0:T(1,128)},...) custom-call(s32[4,8]{1,0:T(4,128)} %bitcast.6, s32[2,8]{1,0:T(2,128)} %bitcast.8, s32[8]{0:T(128)} %flags.3, ...), custom_call_target="tpu_custom_call" | custom-call | tf_op jit(solution)/shard_map/gather/pallas_call | solution.py:587
  151.8 8.7 %product.1 = (bf16[32,256,256]{2,1,0:T(8,128)(2,1)}, f32[1,1]{1,0:T(1,128)}) custom-call(s32[24,1,128]{2,1,0:T(1,128)} %get-tuple-element.10.meta, s32[4,8]{1,0:T(4,128)} %bitcast.7, s32[8]{0:T(128)} %flags.3, f32[128,1,128]{2,1,0:T(1,128)} %get-tuple-element.11.share, bf16[32,256,256]{2,1,0:T(8,128)(2,1)} %get-tuple-element.12.draft, ...), custom_call_target="tpu_custom_call" | custom-call | tf_op jit(solution)/shard_map/product/pallas_call | solution.py:617
